TPU v7x, 32 devices: a whole 2x2x4 slice. The times are simulated.
32 devices in a mesh: tensor: 4 (over z), dp: 4 (over y, core), ctx: 2 (over x).
Axes of the slice: x: 2, y: 2, z: 4, core: 2. Of those that a mesh axis runs over, the one named last changes fastest.
Arguments:
- block_input: bfloat16 [4, 2, 1024, 768], P('dp', 'ctx', 'tensor'), may hold values from -6 to 6
- seq_lengths: int32 [4, 16], P('dp'), may hold values from 0 to 2048, as said below
- project_weight: bfloat16 [2, 768, 2304], P(None, ('dp', 'ctx'), 'tensor'), may hold values from -0.21875 to 0.21875
- project_bias: bfloat16 [2, 2304], P(None, ('tensor', 'dp', 'ctx')), may hold values from -3 to 3
- dense_weight: bfloat16 [2, 768, 768], P(None, ('tensor', 'dp', 'ctx')), may hold values from -0.75 to 0.75
- up_weight: bfloat16 [2, 768, 3072], P(None, ('dp', 'ctx'), 'tensor'), may hold values from -0.21875 to 0.21875
- up_bias: bfloat16 [2, 3072], P(None, ('tensor', 'dp', 'ctx')), may hold values from -3 to 3
- down_weight: bfloat16 [2, 3072, 768], P(None, ('tensor', 'dp', 'ctx')), may hold values from -0.109375 to 0.109375
- norm_gains: bfloat16 [2, 768, 2], replicated, may hold values from 0.5 to 1.5
- shift_vectors: bfloat16 [2, 768, 4], replicated, may hold values from -2 to 2
- cotangent: float32 [4, 2, 1024, 768], P('dp', 'ctx', 'tensor'), may hold values from -6 to 6
Outputs:
- block_output: float32 [4, 2, 1024, 768], P('dp', 'ctx', 'tensor')
- input_grad: float32 [4, 2, 1024, 768], P('dp', 'ctx', 'tensor')
- project_weight_grad: float32 [2, 768, 2304], P(None, ('dp', 'ctx'), 'tensor')
- project_bias_grad: float32 [2, 2304], P(None, ('tensor', 'dp', 'ctx'))
- dense_weight_grad: float32 [2, 768, 768], P(None, ('tensor', 'dp', 'ctx'))
- up_weight_grad: float32 [2, 768, 3072], P(None, ('dp', 'ctx'), 'tensor')
- up_bias_grad: float32 [2, 3072], P(None, ('tensor', 'dp', 'ctx'))
- down_weight_grad: float32 [2, 3072, 768], P(None, ('tensor', 'dp', 'ctx'))
- norm_gains_grad: float32 [2, 768, 2], P(None, ('tensor', 'dp', 'ctx'))
- shift_vectors_grad: float32 [2, 768, 4], P(None, ('tensor', 'dp', 'ctx'))
Inputs may be any that keep to these rules, and one draw needn't show every extreme that they name: `seq_lengths`: each row's entries sum to 2048; its nonzero entries come first, and each of them but the last is 128 or more; a row's slots hold its sequences one after another in this order.
All inputs are finite; a program needn't handle non-finite values.
Results may differ from a plain program's by a relative error of at most 0.018.
Values may be sent and summed in bfloat16 or wider, within the bound.
No kernel may reach another device: no remote copies, remote signals or barrier semaphores. Data moves between devices by JAX's collectives and lax.ppermute only.
A program may use at most 128 MiB of HBM per device.

v0:
```python
from functools import partial

import jax
import jax.numpy as jnp
from jax import lax
from jax.experimental import pallas as pl
from jax.experimental.pallas import tpu as pltpu
from jax.sharding import PartitionSpec as P

HEAD_DIM = 64
ROTARY = 16
LAYERS = 2
EPSILON = 1e-05
MASKED = -1e30
LANES = 128
SCALE = HEAD_DIM ** (-0.5)
FAR = 1 << 24
BF = jnp.bfloat16
F32 = jnp.float32
NT = (((1,), (1,)), ((), ()))


def dot(a, b):
    return jnp.dot(a, b, preferred_element_type=F32)


def dot_nt(a, b):
    return lax.dot_general(a, b, NT, preferred_element_type=F32)


def cost(micros):
    return pl.CostEstimate(
        flops=int(micros * 1.1e9), transcendentals=0, bytes_accessed=int(micros * 3.6e6)
    )


def params(mib=56):
    return pltpu.CompilerParams(vmem_limit_bytes=mib << 20)


def z_gather(own):
    n = lax.axis_size("tensor")
    return [own] + [
        lax.ppermute(own, "tensor", [(s, (s - c) % n) for s in range(n)]) for c in range(1, n)
    ]


def z_scatter(parts):
    n = lax.axis_size("tensor")
    return [parts[0]] + [
        lax.ppermute(parts[c], "tensor", [(s, (s + c) % n) for s in range(n)]) for c in range(1, n)
    ]


def after(value, *needed):
    return lax.optimization_barrier((value,) + needed)[0]


def bits_of(axis):
    return lax.axis_size(axis).bit_length() - 1


def power_of_two():
    sizes = [lax.axis_size(axis) for axis in ("tensor", "dp", "ctx")]
    return sizes[1] > 1 and all(size & (size - 1) == 0 for size in sizes)


def flip(send, step):
    axis, bit = step
    return lax.ppermute(send, axis, [(s, s ^ (1 << bit)) for s in range(lax.axis_size(axis))])


class Scatter:
    def __init__(self, value, first_y, axes=("dp", "ctx"), wire=BF):
        self.labels = [(axis, b) for axis in axes for b in reversed(range(bits_of(axis)))]
        y_steps = [("dp", b) for b in range(1, bits_of("dp"))]
        x_steps = [("ctx", b) for b in range(bits_of("ctx"))]
        self.order = [("tensor", b) for b in range(bits_of("tensor"))] if "tensor" in axes else []
        self.order += [("dp", 0)] + (y_steps + x_steps if first_y else x_steps + y_steps)
        if not isinstance(value, tuple):
            value = value.reshape((2,) * len(self.labels) + value.shape[len(axes) - 1 :])
        self.value, self.wire = value, wire

    def send(self):
        self.step = self.order.pop(0)
        axis, bit = self.step
        dim = self.labels.index(self.step)
        self.labels.pop(dim)
        if isinstance(self.value, tuple):
            lead = (2,) * len(self.labels)
            out, self.keep = (v.reshape(lead + v.shape[1:]) for v in self.value)
            return out
        mine = (lax.axis_index(axis) >> bit) & 1
        self.keep = lax.dynamic_index_in_dim(self.value, mine, dim, keepdims=False)
        out = lax.dynamic_index_in_dim(self.value, 1 - mine, dim, keepdims=False)
        return out.astype(self.wire)

    def receive(self, got):
        self.value = self.keep + got.astype(F32)


def advance(streams, *needed):
    streams = [stream for stream in streams if stream.order]
    sends = lax.optimization_barrier(tuple(stream.send() for stream in streams) + needed)
    gots = [flip(send, stream.step) for send, stream in zip(sends, streams)]
    for stream, got in zip(streams, gots):
        stream.receive(got)


def rotated(tile, cosine, sine_a, sine_b):
    return tile * cosine + pltpu.roll(tile, LANES - 8, 1) * sine_a + pltpu.roll(tile, 8, 1) * sine_b


def unrotated(tile, cosine, sine_a, sine_b):
    return tile * cosine - pltpu.roll(tile, LANES - 8, 1) * sine_a - pltpu.roll(tile, 8, 1) * sine_b


def unit_of(x):
    values = x.astype(F32)
    centre = values - jnp.mean(values, axis=-1, keepdims=True)
    inverse = lax.rsqrt(jnp.mean(centre * centre, axis=-1, keepdims=True) + EPSILON)
    return centre * inverse


def gathered_row(tail_ref, row, own):
    shards = tail_ref.shape[0]
    return jnp.concatenate(
        [tail_ref[s].astype(F32)[row : row + 1, :own] for s in range(shards)], axis=1
    )


def mix_kernel(n, heads, own, *refs):
    chunk_refs = refs[:n]
    mix_ref, tail_ref, vec_ref, cos_ref, sa_ref, sb_ref = refs[n : n + 6]
    xs_ref, first_ref, q_ref, kv_ref, bias_s = refs[-5:]
    load_chunk(chunk_refs, xs_ref.at[0])
    width = xs_ref.shape[-1]

    @pl.when(pl.program_id(0) == 0)
    def _():
        raw = gathered_row(tail_ref, 1, own)
        size = 3 * HEAD_DIM
        pieces = [raw[:, h * size + HEAD_DIM : (h + 1) * size] for h in range(heads)]
        blank = jnp.zeros((1, HEAD_DIM), F32)
        for h in range(heads):
            pieces += [raw[:, h * size : h * size + HEAD_DIM], blank]
        bias_s[...] = jnp.concatenate(pieces, axis=1)

    first = (unit_of(xs_ref[0]) * vec_ref[0:1] + vec_ref[2:3]).astype(BF)
    first_ref[0] = first
    proj = dot(first, mix_ref[...].reshape(width, -1)[:, : 2 * heads * LANES]) + bias_s[...]
    cosine, sine_a, sine_b = cos_ref[0], sa_ref[0], sb_ref[0]
    for h in range(heads):
        cols = slice(h * LANES, (h + 1) * LANES)
        kv_ref[0, :, cols] = rotated(proj[:, cols], cosine, sine_a, sine_b).astype(BF)
        qcols = slice((heads + h) * LANES, (heads + h + 1) * LANES)
        q_ref[0, :, cols] = (rotated(proj[:, qcols], cosine, sine_a, sine_b) * SCALE).astype(BF)


def store_chunk(refs, value):
    for j, ref in enumerate(refs):

        @pl.when(pl.program_id(0) == j)
        def _(ref=ref):
            ref[...] = value


def load_chunk(refs, held):
    for j, ref in enumerate(refs):

        @pl.when(pl.program_id(0) == j)
        def _(ref=ref):
            held[...] = ref[...]


def feed_kernel(own, *refs):
    x_ref, up_ref, down_ref, tail_ref, vec_ref, second_ref, active_ref, slope_ref = refs[:8]
    part_refs, bias_s = refs[8:-1], refs[-1]

    @pl.when(pl.program_id(0) == 0)
    def _():
        bias_s[...] = gathered_row(tail_ref, 0, own)

    width = x_ref.shape[-1]
    second = (unit_of(x_ref[0]) * vec_ref[1:2] + vec_ref[3:4]).astype(BF)
    second_ref[0] = second
    hidden = dot(second, up_ref[...].reshape(width, -1)) + bias_s[...]
    half = 0.5 * (1.0 + lax.erf(hidden * (0.5**0.5)))
    active = (hidden * half).astype(BF)
    active_ref[0] = active
    bell = jnp.exp(hidden * hidden * -0.5) * 0.3989422804014327
    slope_ref[0] = (half + hidden * bell).astype(BF)
    store_chunk(part_refs, dot(active, down_ref[...].reshape(-1, width)).astype(BF))


def chunk_specs(n, tokens, gathered, k):
    shards, _, ff = gathered.shape
    token = lambda w: pl.BlockSpec((1, tokens, w), lambda c: (c, 0, 0))
    whole = lambda a: pl.BlockSpec(a.shape, lambda c: (0,) * a.ndim)
    weight = lambda j: pl.BlockSpec((shards, k, ff), lambda c: (0, j, 0))
    out = lambda w: jax.ShapeDtypeStruct((n, tokens, w), BF)
    return token, whole, weight, out


def mix_pass(tokens, chunks, place, n, gathered, k, own, vec, tables, heads, held=()):
    width = chunks[0].shape[1]
    count = len(chunks)
    wide = heads * LANES
    shards, _, ff = gathered.shape
    whole = lambda a: pl.BlockSpec(a.shape, lambda c: (0,) * a.ndim)
    token = lambda w: pl.BlockSpec((1, tokens, w), lambda c: (place + c, 0, 0))
    weight = pl.BlockSpec((shards, k, ff), lambda c: (0, 2, 0))
    last = gathered.shape[1] // 8 - 1
    tail = pl.BlockSpec((shards, 8, ff), lambda c: (0, last, 0))
    out = lambda m, w: jax.ShapeDtypeStruct((m, tokens, w), BF)
    first_held = count + 6
    return pl.pallas_call(
        partial(mix_kernel, count, heads, own),
        grid=(count,),
        in_specs=[pl.BlockSpec((tokens, width), lambda c: (0, 0))] * count
        + [weight, tail, whole(vec)]
        + [token(LANES)] * 3
        + [pl.BlockSpec(memory_space=pl.ANY)] * len(held),
        out_specs=[token(width), token(width), token(wide)]
        + [pl.BlockSpec((1, tokens, wide), lambda c: (c, 0, 0))],
        out_shape=[out(n, width), out(n, width), out(n, wide), out(count, wide)],
        input_output_aliases={first_held + i: i for i in range(len(held))},
        scratch_shapes=[pltpu.VMEM((1, 2 * wide), F32)],
        compiler_params=params(),
        cost_estimate=cost(12),
        name="mix_pass",
    )(*chunks, gathered, gathered, vec, *tables, *held)


def feed_pass(xs, gathered, k, own, vec):
    n, tokens, width = xs.shape
    ff = gathered.shape[2]
    token, whole, weight, out = chunk_specs(n, tokens, gathered, k)
    last = gathered.shape[1] // 8 - 1
    second, active, slope, *parts = pl.pallas_call(
        partial(feed_kernel, own),
        grid=(n,),
        in_specs=[token(width), weight(0), weight(1)]
        + [pl.BlockSpec((gathered.shape[0], 8, ff), lambda c: (0, last, 0)), whole(vec)],
        out_specs=[token(width), token(ff), token(ff)]
        + [pl.BlockSpec((tokens, width), lambda c: (0, 0))] * n,
        out_shape=[out(width), out(ff), out(ff)]
        + [jax.ShapeDtypeStruct((tokens, width), BF)] * n,
        scratch_shapes=[pltpu.VMEM((1, ff), F32)],
        compiler_params=params(),
        cost_estimate=cost(20),
        name="feed_pass",
    )(xs, gathered, gathered, gathered, vec)
    return second, active, slope, parts


def middle_kernel(n, me_ref, dense_ref, grads_ref, *refs):
    mixed_refs, part_refs = refs[:n], refs[n : 2 * n]
    do_refs, out_refs = refs[2 * n : 3 * n], refs[3 * n :]
    rows = mixed_refs[0].shape[1] // dense_ref.shape[0]
    dense = dense_ref[:, :rows].reshape(-1, dense_ref.shape[-1])
    for c in range(n):
        total = dot(mixed_refs[c][...], dense) + part_refs[c][...].astype(F32)
        out_refs[c][...] = total.astype(BF)
        grad = grads_ref[lax.rem(me_ref[0] + c, n)]
        do_refs[c][...] = dot_nt(grad, dense).astype(BF)


def middle(me1, mixed, gathered, k, d, parts, grads):
    n = len(parts)
    padded = d + -d % 8
    full = lambda a: pl.BlockSpec(a.shape, lambda i: (0,) * a.ndim)
    dense = pl.BlockSpec(
        (gathered.shape[0], padded, gathered.shape[2]), lambda i: (0, 3 * k // padded, 0)
    )
    outs = pl.pallas_call(
        partial(middle_kernel, n),
        grid=(1,),
        in_specs=[pl.BlockSpec(memory_space=pltpu.SMEM), dense, full(grads)]
        + [full(a) for a in mixed + parts],
        out_specs=[full(a) for a in mixed + parts],
        out_shape=[jax.ShapeDtypeStruct(mixed[0].shape, BF)] * n
        + [jax.ShapeDtypeStruct(parts[0].shape, BF)] * n,
        compiler_params=params(),
        cost_estimate=cost(4),
        name="middle",
    )(me1, gathered, grads, *mixed, *parts)
    return outs[:n], outs[n:]


def load_pairs(kv_refs, kv_s):
    place = 0
    for ref in kv_refs:
        for c in range(ref.shape[0]):
            kv_s[place] = ref[c, 0]
            place += 1


def each_block(plan_ref, row, c, blocks, take):
    start = c * (blocks + 1)
    count = plan_ref[row, start]

    def pair(t, _):
        take([plan_ref[row, start + 1 + 2 * t], plan_ref[row, start + 2 + 2 * t]])
        return 0

    lax.fori_loop(0, count // 2, pair, 0)

    @pl.when(count % 2 == 1)
    def _():
        take([plan_ref[row, start + count]])


def allowed_pairs(base_ref, begin_ref, kb, c, n, shape):
    key_slot = base_ref[n + kb] + lax.broadcasted_iota(jnp.int32, shape, 0)
    query_slot = base_ref[c] + lax.broadcasted_iota(jnp.int32, shape, 1)
    return (key_slot >= begin_ref[0, c]) & (key_slot <= query_slot)


def attend_kernel(heads, extras, groups, need_ref, base_ref, begin_ref, q_ref, *refs):
    kv_refs = refs[:groups]
    n, _, count, _ = q_ref.shape
    mixed_refs = refs[groups : groups + n]
    ot_ref, lse_ref, kv_s, vt_s, top_s, total_s, acc_s, mixed_s = refs[groups + n :]
    blocks = n * (1 + extras)
    row = pl.program_id(0)
    load_pairs(kv_refs, kv_s)

    def turn(kb, _):
        for h in range(heads):
            tile = kv_s[kb, :, h * LANES : (h + 1) * LANES].astype(F32)
            vt_s[kb, h] = tile.T[HEAD_DIM:].astype(BF)
        return 0

    lax.fori_loop(0, blocks, turn, 0)

    def per_query(c, _):
        top_s[...] = jnp.full(top_s.shape, MASKED, F32)
        total_s[...] = jnp.zeros(total_s.shape, F32)
        acc_s[...] = jnp.zeros(acc_s.shape, F32)

        def take(kbs):
            column = lambda h: slice(h * LANES, (h + 1) * LANES)
            held = [
                [dot_nt(kv_s[kb, :, column(h)], q_ref[c, 0, :, column(h)]) for h in range(heads)]
                for kb in kbs
            ]
            masks = [allowed_pairs(base_ref, begin_ref, kb, c, n, (count, count)) for kb in kbs]
            low, fades = [], []
            for h in range(heads):
                scores = [jnp.where(mask, own[h], MASKED) for mask, own in zip(masks, held)]
                old = top_s[h]
                new = old
                for score in scores:
                    new = jnp.maximum(new, jnp.max(score, axis=0, keepdims=True))
                fade = jnp.exp(old - new)
                total = total_s[h] * fade
                weights = []
                for score in scores:
                    weight = jnp.exp(score - new)
                    total = total + jnp.sum(weight, axis=0, keepdims=True)
                    weights.append(weight.astype(BF))
                top_s[h] = new
                total_s[h] = total
                low.append(weights)
                fades.append(fade)
            for h in range(heads):
                acc = acc_s[h] * fades[h]
                for kb, weight in zip(kbs, low[h]):
                    acc = acc + dot(vt_s[kb, h], weight)
                acc_s[h] = acc

        each_block(need_ref, row, c, blocks, take)
        outs = []
        for h in range(heads):
            total = total_s[h]
            outs.append(acc_s[h] / total)
            lse_ref[0, c, h : h + 1] = top_s[h] + jnp.log(total)
        whole = jnp.concatenate(outs, axis=0)
        ot_ref[0, c] = whole
        mixed_s[c] = whole.T.astype(BF)
        return 0

    lax.fori_loop(0, n, per_query, 0)
    for c in range(n):
        mixed_refs[c][0] = mixed_s[c]


def attention_specs(q, kvs):
    n, rows, count, wide = q.shape
    smem = pl.BlockSpec(memory_space=pltpu.SMEM)
    begin = pl.BlockSpec((1, n, 1, count), lambda r: (r, 0, 0, 0))
    tokens = lambda a: pl.BlockSpec((a.shape[0], 1, count, wide), lambda r: (0, r, 0, 0))
    flat = [a for group in kvs for a in group]
    return n, rows, count, wide, smem, begin, tokens, flat


def attend(need, base, begin, q, kvs, heads):
    extras = len(kvs) - 1
    n, rows, count, wide, smem, begin_spec, tokens, flat = attention_specs(q, kvs)
    blocks = n * (1 + extras)
    narrow = heads * HEAD_DIM
    outs = pl.pallas_call(
        partial(attend_kernel, heads, extras, len(flat)),
        grid=(rows,),
        in_specs=[smem, smem, begin_spec, tokens(q)] + [tokens(a) for a in flat],
        out_specs=[pl.BlockSpec((1, count, narrow), lambda r: (r, 0, 0))] * n
        + [
            pl.BlockSpec((1, n, narrow, count), lambda r: (r, 0, 0, 0)),
            pl.BlockSpec((1, n, heads, count), lambda r: (r, 0, 0, 0)),
        ],
        out_shape=[jax.ShapeDtypeStruct((rows, count, narrow), BF)] * n
        + [
            jax.ShapeDtypeStruct((rows, n, narrow, count), F32),
            jax.ShapeDtypeStruct((rows, n, heads, count), F32),
        ],
        scratch_shapes=[
            pltpu.VMEM((blocks, count, wide), BF),
            pltpu.VMEM((blocks, heads, HEAD_DIM, count), BF),
            pltpu.VMEM((heads, 1, count), F32),
            pltpu.VMEM((heads, 1, count), F32),
            pltpu.VMEM((heads, HEAD_DIM, count), F32),
            pltpu.VMEM((n, count, narrow), BF),
        ],
        compiler_params=params(),
        cost_estimate=cost(400),
        name="attend",
    )(need, base, begin, q, *flat)
    return [a.reshape(rows * count, narrow) for a in outs[:n]], outs[n], outs[n + 1]


def attend_back_kernel(heads, extras, groups, need_ref, base_ref, begin_ref, q_ref, *refs):
    n, _, count, _ = q_ref.shape
    do_refs, lse_ref, ot_ref = refs[:n], refs[n], refs[n + 1]
    kv_refs = refs[n + 2 : n + 2 + groups]
    dq_ref = refs[n + 2 + groups]
    dkv_refs = refs[n + 3 + groups : n + 4 + groups + extras]
    kv_s, kt_s, dkv_s, dqt_s, delta_s, do_s, narrow_s = refs[n + 4 + groups + extras :]
    blocks = n * (1 + extras)
    row = pl.program_id(0)
    load_pairs(kv_refs, kv_s)
    for c in range(n):
        narrow_s[c] = do_refs[c][0]

    def turn(kb, _):
        for h in range(heads):
            tile = kv_s[kb, :, h * LANES : (h + 1) * LANES].astype(F32)
            kt_s[kb, h] = tile.T[:HEAD_DIM].astype(BF)
        dkv_s[kb] = jnp.zeros(dkv_s.shape[1:], F32)
        return 0

    lax.fori_loop(0, blocks, turn, 0)

    def per_query(c, _):
        dqt_s[...] = jnp.zeros(dqt_s.shape, F32)
        for h in range(heads):
            cols = slice(h * LANES, (h + 1) * LANES)
            grad = narrow_s[c, :, h * HEAD_DIM : (h + 1) * HEAD_DIM].astype(F32)
            grad = jnp.concatenate([jnp.zeros((count, HEAD_DIM), F32), grad], axis=1)
            do_s[:, cols] = grad.astype(BF)
            dot_t = grad.T[HEAD_DIM:]
            out_t = ot_ref[0, c, h * HEAD_DIM : (h + 1) * HEAD_DIM]
            delta_s[h] = jnp.sum(dot_t * out_t, axis=0, keepdims=True)

        def take(kbs):
            column = lambda h: slice(h * LANES, (h + 1) * LANES)
            queries = [q_ref[c, 0, :, column(h)] for h in range(heads)]
            grads = [do_s[:, column(h)] for h in range(heads)]
            held = []
            for kb in kbs:
                pairs = [kv_s[kb, :, column(h)] for h in range(heads)]
                held.append(
                    [(dot_nt(pairs[h], queries[h]), dot_nt(pairs[h], grads[h])) for h in range(heads)]
                )
            low = []
            for kb, own in zip(kbs, held):
                allowed = allowed_pairs(base_ref, begin_ref, kb, c, n, (count, count))
                for h in range(heads):
                    scores = jnp.where(allowed, own[h][0], MASKED)
                    probs = jnp.exp(scores - lse_ref[0, c, h : h + 1])
                    steps = probs * (own[h][1] - delta_s[h])
                    low.append((steps.astype(BF), probs.astype(BF)))
            for i, kb in enumerate(kbs):
                for h in range(heads):
                    steps, probs = low[i * heads + h]
                    dqt_s[h] += dot(kt_s[kb, h], steps)
                    dkv_s[kb, :, column(h)] += dot(steps, queries[h]) + dot(probs, grads[h])

        each_block(need_ref, row, c, blocks, take)
        for h in range(heads):
            tile = jnp.concatenate([dqt_s[h], jnp.zeros((HEAD_DIM, count), F32)], axis=0)
            dq_ref[c, 0, :, h * LANES : (h + 1) * LANES] = tile.T * SCALE
        return 0

    lax.fori_loop(0, n, per_query, 0)
    for e, ref in enumerate(dkv_refs):
        for c in range(n):
            ref[c, 0] = dkv_s[e * n + c].astype(ref.dtype)


def attend_back(need, base, begin, q, do, lse, ot, kvs, heads):
    extras = len(kvs) - 1
    n, rows, count, wide, smem, begin_spec, tokens, flat = attention_specs(q, kvs)
    blocks = n * (1 + extras)
    narrow = heads * HEAD_DIM
    return pl.pallas_call(
        partial(attend_back_kernel, heads, extras, len(flat)),
        grid=(rows,),
        in_specs=[smem, smem, begin_spec, tokens(q)]
        + [pl.BlockSpec((1, count, narrow), lambda r: (r, 0, 0))] * n
        + [
            pl.BlockSpec((1, n, heads, count), lambda r: (r, 0, 0, 0)),
            pl.BlockSpec((1, n, narrow, count), lambda r: (r, 0, 0, 0)),
        ]
        + [tokens(a) for a in flat],
        out_specs=[tokens(q)] * (2 + extras),
        out_shape=[jax.ShapeDtypeStruct(q.shape, F32)] * 2
        + [jax.ShapeDtypeStruct(q.shape, BF)] * extras,
        scratch_shapes=[
            pltpu.VMEM((blocks, count, wide), BF),
            pltpu.VMEM((blocks, heads, HEAD_DIM, count), BF),
            pltpu.VMEM((blocks, count, wide), F32),
            pltpu.VMEM((heads, HEAD_DIM, count), F32),
            pltpu.VMEM((heads, 1, count), F32),
            pltpu.VMEM((count, wide), BF),
            pltpu.VMEM((n, count, narrow), BF),
        ],
        compiler_params=params(),
        cost_estimate=cost(40),
        name="attend_back",
    )(need, base, begin, q, *[a.reshape(rows, count, narrow) for a in do], lse, ot, *flat)


TN = (((0,), (0,)), ((), ()))


def dot_tn(a, b):
    return lax.dot_general(a, b, TN, preferred_element_type=F32)


def half_shard(place, inner, bit):
    return (place // inner * 2 + bit) * inner + place % inner


def store_shards(refs, core_ref, shards, inner, block):
    if len(refs) == 1:
        for s in range(shards):
            refs[0][s] = block(s)
        return
    mine = core_ref[0]
    for place in range(shards // 2):
        refs[0][place] = block(half_shard(place, inner, 1 - mine))
        refs[1][place] = block(half_shard(place, inner, mine))


def row_block(ref, s, size):
    start = s * size if isinstance(s, int) else pl.multiple_of(s * size, 8)
    return ref[pl.ds(start, size)]


def feed_back_kernel(n, gates, inner, split, core_ref, *refs):
    grad_refs = refs[:n]
    x_ref, slope_ref, second_ref, active_ref, up_ref, down_ref, vec_ref = refs[n : n + 7]
    refs = refs[n + 7 + gates :]
    scaled_ref, sums_ref, outs = refs[0], refs[1], refs[2:-4]
    up_s, down_s, grad_s, tail_s = refs[-4:]
    width = x_ref.shape[-1]
    last = pl.program_id(0) == pl.num_programs(0) - 1

    @pl.when(pl.program_id(0) == 0)
    def _():
        sums_ref[...] = jnp.zeros(sums_ref.shape, F32)
        up_s[...] = jnp.zeros(up_s.shape, F32)
        down_s[...] = jnp.zeros(down_s.shape, F32)

    load_chunk(grad_refs, grad_s)
    down = down_ref[...].reshape(-1, width)
    grad = grad_s[...]
    grad_active = dot_nt(grad, down)
    down_s[...] += dot_tn(active_ref[0], grad)
    grad_hidden = (grad_active * slope_ref[0].astype(F32)).astype(BF)
    grad_second = dot_nt(grad_hidden, up_ref[...].reshape(width, -1))
    unit = unit_of(x_ref[0])
    sums_ref[0:1] += jnp.sum(grad_second * unit, axis=0, keepdims=True)
    sums_ref[1:2] += jnp.sum(grad_second, axis=0, keepdims=True)
    sums_ref[2:3] += jnp.sum(grad_hidden.astype(F32), axis=0, keepdims=True)
    scaled_ref[0] = grad_second * vec_ref[1:2]
    up_s[...] += dot_tn(second_ref[0], grad_hidden)

    @pl.when(last)
    def _():
        shards, k = up_ref.shape[:2]
        f = down_s.shape[0] // shards
        own = up_s.shape[1] // shards
        pad = jnp.zeros((8, width - own), F32)
        for s in range(shards):
            tail = jnp.broadcast_to(sums_ref[2:3, s * own : (s + 1) * own], (8, own))
            tail_s[s] = jnp.concatenate([tail, pad], axis=1)
        up_block = lambda s: row_block(up_s, s, k).astype(BF)
        rest_block = lambda s: jnp.concatenate(
            [row_block(down_s, s, f), tail_s[s]], axis=0
        ).astype(BF)
        if split:
            store_shards(outs[:2], core_ref, shards, inner, up_block)
            store_shards(outs[2:], core_ref, shards, inner, rest_block)
        else:
            store_shards(
                outs, core_ref, shards, inner,
                lambda s: jnp.concatenate([up_block(s), rest_block(s)], axis=0),
            )


def feed_back(core1, gs, xs, slope, second, active, gathered, k, vec, inner, split, gates=()):
    n, tokens, width = xs.shape
    shards, _, ff = gathered.shape
    f = ff // shards
    token, whole, weight, _ = chunk_specs(n, tokens, gathered, k)
    fixed = pl.BlockSpec((8, width), lambda c: (0, 0))
    grads = [(shards, k + f + 8, width)]
    if split:
        grads = [(shards // 2, k, width)] * 2 + [(shards // 2, f + 8, width)] * 2
    return pl.pallas_call(
        partial(feed_back_kernel, n, len(gates), inner, split),
        grid=(n,),
        in_specs=[pl.BlockSpec(memory_space=pltpu.SMEM)]
        + [whole(gs[0])] * n
        + [token(width), token(ff), token(width), token(ff), weight(0), weight(1), fixed]
        + [pl.BlockSpec(memory_space=pl.ANY)] * len(gates),
        out_specs=[token(width), fixed] + [pl.BlockSpec(g, lambda c: (0, 0, 0)) for g in grads],
        scratch_shapes=[
            pltpu.VMEM((width, ff), F32),
            pltpu.VMEM((ff, width), F32),
            pltpu.VMEM((tokens, width), BF),
            pltpu.VMEM((shards, 8, width), F32),
        ],
        out_shape=[
            jax.ShapeDtypeStruct((n, tokens, width), F32),
            jax.ShapeDtypeStruct((8, width), F32),
        ]
        + [jax.ShapeDtypeStruct(g, BF) for g in grads],
        compiler_params=params(),
        cost_estimate=cost(12),
        name="feed_back",
    )(core1, *gs, xs, slope, second, active, gathered, gathered, vec, *gates)


def mix_back_kernel(n, inner, outs, core_ref, *refs):
    first_ref, gp_ref, bias_ref = refs[:3]
    mixed_refs, grad_refs = refs[3 : 3 + n], refs[3 + n : 3 + 2 * n]
    grads_refs = refs[-4 - outs : -4]
    mix_s, dense_s, mixed_s, grad_s = refs[-4:]
    last = pl.program_id(0) == pl.num_programs(0) - 1

    @pl.when(pl.program_id(0) == 0)
    def _():
        mix_s[...] = jnp.zeros(mix_s.shape, F32)
        dense_s[...] = jnp.zeros(dense_s.shape, F32)

    load_chunk(grad_refs, grad_s)
    load_chunk(mixed_refs, mixed_s)
    mix_s[...] += dot_tn(first_ref[0], gp_ref[0])
    dense_s[...] += dot_tn(mixed_s[...], grad_s[...])

    @pl.when(last)
    def _():
        shards = bias_ref.shape[0]
        k = mix_s.shape[0] // shards
        d = dense_s.shape[0] // shards

        def block(s):
            rows = [row_block(mix_s, s, k), row_block(dense_s, s, d), bias_ref[s]]
            return jnp.concatenate(rows, axis=0).astype(BF)

        store_shards(grads_refs, core_ref, shards, inner, block)


def mix_back(core1, first, gp, mixed, gs, bias, inner, split, micros, gates=()):
    n, tokens, width = first.shape
    shards = bias.shape[0]
    narrow = mixed[0].shape[-1]
    token = lambda w: pl.BlockSpec((1, tokens, w), lambda c: (c, 0, 0))
    whole = lambda a: pl.BlockSpec(a.shape, lambda c: (0,) * a.ndim)
    count = 2 if split else 1
    grads = (shards // count, width // shards + narrow // shards + 8, width)
    return pl.pallas_call(
        partial(mix_back_kernel, n, inner, count),
        grid=(n,),
        in_specs=[pl.BlockSpec(memory_space=pltpu.SMEM), token(width), token(gp.shape[-1]), whole(bias)]
        + [whole(mixed[0])] * n
        + [whole(gs[0])] * n
        + [pl.BlockSpec(memory_space=pl.ANY)] * len(gates),
        out_specs=[pl.BlockSpec(grads, lambda c: (0, 0, 0))] * count,
        scratch_shapes=[
            pltpu.VMEM((width, gp.shape[-1]), F32),
            pltpu.VMEM((narrow, width), F32),
            pltpu.VMEM((tokens, narrow), BF),
            pltpu.VMEM((tokens, width), BF),
        ],
        out_shape=[jax.ShapeDtypeStruct(grads, BF)] * count,
        compiler_params=params(),
        cost_estimate=cost(micros),
        name="mix_back",
    )(core1, first, gp, bias, *mixed, *gs, *gates)


def join_kernel(n, me_ref, dense_ref, residual_ref, vec_ref, *refs):
    mixed_refs, share_refs, out_ref, sent_ref = refs[:n], refs[n : 2 * n], refs[2 * n], refs[2 * n + 1]
    total = residual_ref[...] + vec_ref[4:5] + vec_ref[5:6]
    for c in range(n):
        rows = dense_ref[:, (n - c) % n]
        rows = rows.reshape(-1, rows.shape[-1])
        total = total + share_refs[c][...].astype(F32) + dot(mixed_refs[c][...], rows)
    out_ref[...] = total
    sent_ref[...] = total.astype(BF)


def join(me1, mixed, dense_all, shares, residual, vec):
    shape = residual.shape
    vmem = pl.BlockSpec(memory_space=pltpu.VMEM)
    return pl.pallas_call(
        partial(join_kernel, len(shares)),
        in_specs=[pl.BlockSpec(memory_space=pltpu.SMEM)] + [vmem] * (3 + 2 * len(shares)),
        out_specs=[vmem, vmem],
        out_shape=[jax.ShapeDtypeStruct(shape, F32), jax.ShapeDtypeStruct(shape, BF)],
        compiler_params=params(),
        cost_estimate=cost(3),
        name="join",
    )(me1, dense_all, residual, vec, *mixed, *shares)


def turn_kernel(n, gates, me_ref, *refs):
    summed = refs[0][...].astype(F32)
    for ref in refs[1:n]:
        summed = summed + ref[...].astype(F32)
    grad_ref, x_ref = refs[n : n + 2]
    refs = refs[n + 2 :]
    values = x_ref[...].astype(F32)
    centre = values - jnp.mean(values, axis=-1, keepdims=True)
    inverse = lax.rsqrt(jnp.mean(centre * centre, axis=-1, keepdims=True) + EPSILON)
    unit = centre * inverse
    mean_s = jnp.mean(summed, axis=-1, keepdims=True)
    mean_su = jnp.mean(summed * unit, axis=-1, keepdims=True)
    grad = grad_ref[...] + inverse * (summed - mean_s - unit * mean_su)
    if len(refs) == gates + 1:
        refs[-1][...] = grad
        return
    dense_ref, out_ref, sent_ref, sums_ref = refs[0], *refs[gates + 1 : gates + 4]
    piece_refs = refs[gates + 4 :]
    out_ref[...] = grad
    sent = grad.astype(BF)
    sent_ref[...] = sent
    for c, piece_ref in enumerate(piece_refs):
        rows = dense_ref[:, c]
        piece_ref[...] = dot_nt(sent, rows.reshape(-1, rows.shape[-1])).astype(BF)
    sums_ref[0:1] = jnp.sum(grad, axis=0, keepdims=True)
    sums_ref[1:2] = jnp.sum(grad_ref[...], axis=0, keepdims=True)


def turn(me1, parts, grad, x_own, dense_all=None, gates=()):
    shape = grad.shape
    outs = [jax.ShapeDtypeStruct(shape, F32)]
    vmem = pl.BlockSpec(memory_space=pltpu.VMEM)
    more = []
    if dense_all is not None:
        more = [dense_all]
        outs += [jax.ShapeDtypeStruct(shape, BF), jax.ShapeDtypeStruct((8, shape[1]), F32)]
        narrow = dense_all.shape[0] * dense_all.shape[2]
        outs += [jax.ShapeDtypeStruct((shape[0], narrow), BF)] * dense_all.shape[1]
    return pl.pallas_call(
        partial(turn_kernel, len(parts), len(gates)),
        in_specs=[pl.BlockSpec(memory_space=pltpu.SMEM)]
        + [vmem] * (len(parts) + 2 + len(more))
        + [pl.BlockSpec(memory_space=pl.ANY)] * len(gates),
        out_specs=[vmem] * len(outs),
        out_shape=outs,
        compiler_params=params(),
        cost_estimate=cost(3),
        name="turn",
    )(me1, *parts, grad, x_own, *more, *gates)


def exit_kernel(n, heads, extras, gates, inner, outs, halves, _, core_ref, dq_ref, dkv_ref, *refs):
    got_refs = refs[:extras]
    cos_ref, sa_ref, sb_ref, x_ref, mix_ref, vec_ref, scaled_ref = refs[extras : extras + 7]
    refs = refs[extras + 7 :]
    fold = halves > 0
    if fold:
        first_ref, mixed_refs, grad_refs = refs[0], refs[1 : 1 + n], refs[1 + n : 1 + 2 * n]
        refs = refs[1 + 2 * n :]
    refs = refs[gates:]
    gp_ref, sums_ref, part_refs = refs[0], refs[1], refs[2 : 2 + outs]
    grads_refs, scratch = refs[2 + outs : 2 + outs + halves], refs[2 + outs + halves :]
    width = x_ref.shape[-1]

    @pl.when(pl.program_id(0) == 0)
    def _():
        sums_ref[...] = jnp.zeros(sums_ref.shape, F32)
        if fold:
            scratch[0][...] = jnp.zeros(scratch[0].shape, F32)
            scratch[1][...] = jnp.zeros(scratch[1].shape, F32)

    if fold:
        mix_s, dense_s, mixed_s, grad_s, tail_s = scratch
        load_chunk(grad_refs, grad_s)
        load_chunk(mixed_refs, mixed_s)
        dense_s[...] += dot_tn(mixed_s[...], grad_s[...])
    cosine, sine_a, sine_b = cos_ref[0], sa_ref[0], sb_ref[0]
    for h in range(heads):
        cols = slice(h * LANES, (h + 1) * LANES)
        pair = dkv_ref[0, :, cols]
        for ref in got_refs:
            pair = pair + ref[0, :, cols].astype(F32)
        gp_ref[0, :, cols] = unrotated(pair, cosine, sine_a, sine_b).astype(BF)
        qcols = slice((heads + h) * LANES, (heads + h + 1) * LANES)
        gp_ref[0, :, qcols] = unrotated(dq_ref[0, :, cols], cosine, sine_a, sine_b).astype(BF)
    gp = gp_ref[0]
    grad_first = dot_nt(gp, mix_ref[...].reshape(width, -1))
    if fold:
        mix_s[...] += dot_tn(first_ref[0], gp)
    unit = unit_of(x_ref[0])
    sums_ref[0:1] += jnp.sum(grad_first * unit, axis=0, keepdims=True)
    sums_ref[1:2] += jnp.sum(grad_first, axis=0, keepdims=True)
    sums_ref[2:3] += jnp.sum(gp.astype(F32), axis=0, keepdims=True)
    part = (grad_first * vec_ref[0:1] + scaled_ref[0]).astype(BF)
    if outs == 1:
        part_refs[0][0] = part
    else:
        store_chunk(part_refs, part)
    if not fold:
        return

    @pl.when(pl.program_id(0) == pl.num_programs(0) - 1)
    def _():
        shards = mix_ref.shape[0]
        k = mix_s.shape[0] // shards
        d = dense_s.shape[0] // shards
        row = sums_ref[2:3]
        pieces = []
        for h in range(heads):
            query = (heads + h) * LANES
            pieces.append(row[:, query : query + HEAD_DIM])
            pieces.append(row[:, h * LANES : (h + 1) * LANES])
        raw = jnp.concatenate(pieces, axis=1)
        own = raw.shape[1] // shards
        pad = jnp.zeros((8, width - own), F32)
        for s in range(shards):
            tail = jnp.broadcast_to(raw[:, s * own : (s + 1) * own], (8, own))
            tail_s[s] = jnp.concatenate([tail, pad], axis=1)

        def block(s):
            rows = [row_block(mix_s, s, k), row_block(dense_s, s, d), tail_s[s]]
            return jnp.concatenate(rows, axis=0).astype(BF)

        store_shards(grads_refs, core_ref, shards, inner, block)


def exit_pass(
    me1, core1, dq, dkv, got, tables, xs, gathered, k, vec, scaled, heads, inner, halves=0,
    fold=(), gates=(),
):
    n, tokens, width = xs.shape
    shards, _, ff = gathered.shape
    wide = heads * LANES
    narrow = heads * HEAD_DIM
    token = lambda w: pl.BlockSpec((1, tokens, w), lambda c, s: (c, 0, 0))
    weight = lambda j: pl.BlockSpec((shards, k, ff), lambda c, s: (0, j, 0))
    whole = lambda a: pl.BlockSpec(a.shape, lambda c, s: (0,) * a.ndim)
    fixed = pl.BlockSpec((8, width), lambda c, s: (0, 0))
    flat = lambda a: a.reshape(n, tokens, wide)
    fold_specs, grad_specs, grad_shapes, scratch = [], [], [], []
    if halves:
        part_specs = [pl.BlockSpec((1, tokens, width), lambda c, s: ((s[0] + c) % n, 0, 0))]
        part_shapes = [jax.ShapeDtypeStruct((n, tokens, width), BF)]
        fold_specs = [token(width)] + [whole(a) for a in fold[1:]]
        grads = (shards // halves, width // shards + narrow // shards + 8, width)
        grad_specs = [pl.BlockSpec(grads, lambda c, s: (0, 0, 0))] * halves
        grad_shapes = [jax.ShapeDtypeStruct(grads, BF)] * halves
        scratch = [
            pltpu.VMEM((width, 2 * wide), F32),
            pltpu.VMEM((narrow, width), F32),
            pltpu.VMEM((tokens, narrow), BF),
            pltpu.VMEM((tokens, width), BF),
            pltpu.VMEM((shards, 8, width), F32),
        ]
    else:
        part_specs = [pl.BlockSpec((tokens, width), lambda c, s: (0, 0))] * n
        part_shapes = [jax.ShapeDtypeStruct((tokens, width), BF)] * n
    outs = len(part_specs)
    gp, sums, *rest = pl.pallas_call(
        partial(exit_kernel, n, heads, len(got), len(gates), inner, outs, halves),
        grid_spec=pltpu.PrefetchScalarGridSpec(
            num_scalar_prefetch=1,
            grid=(n,),
            in_specs=[pl.BlockSpec(memory_space=pltpu.SMEM)]
            + [token(wide)] * (2 + len(got))
            + [token(LANES)] * 3
            + [token(width), weight(2), fixed, token(width)]
            + fold_specs
            + [pl.BlockSpec(memory_space=pl.ANY)] * len(gates),
            out_specs=[token(2 * wide), fixed] + part_specs + grad_specs,
            scratch_shapes=scratch,
        ),
        out_shape=[
            jax.ShapeDtypeStruct((n, tokens, 2 * wide), BF),
            jax.ShapeDtypeStruct((8, width), F32),
        ]
        + part_shapes
        + grad_shapes,
        compiler_params=params(),
        cost_estimate=cost(100),
        name="exit_pass",
    )(
        me1, core1, flat(dq), flat(dkv), *[flat(a) for a in got], *tables, xs, gathered, vec,
        scaled, *fold, *gates,
    )
    return gp, rest[:outs], sums, tuple(rest[outs:])


def mix_columns(weight, heads):
    lead = weight.shape[:-1]
    split = weight.reshape(lead + (heads, 3, HEAD_DIM))
    pairs = split[..., 1:, :].reshape(lead + (heads * LANES,))
    query = jnp.concatenate([split[..., 0, :], jnp.zeros_like(split[..., 0, :])], axis=-1)
    return jnp.concatenate([pairs, query.reshape(lead + (heads * LANES,))], axis=-1)


def unmix_columns(grad, heads):
    lead = grad.shape[:-1]
    split = grad.reshape(lead + (2, heads, 2, HEAD_DIM))
    order = [split[..., 1, :, 0, :], split[..., 0, :, 0, :], split[..., 0, :, 1, :]]
    return jnp.stack(order, axis=-2).reshape(lead + (heads * 3 * HEAD_DIM,))


def pack_layer(mix_w, mix_b, dense_w, up_w, up_b, down_w, heads):
    width = up_w.shape[1]
    mix = mix_columns(mix_w, heads)
    wide = lambda v: jnp.pad(v, (0, width - v.shape[0]))[None]
    rows = [up_w, down_w, jnp.pad(mix, ((0, 0), (0, width - mix.shape[1])))]
    if dense_w is not None:
        rows += [dense_w, jnp.zeros((-dense_w.shape[0] % 8, width), up_w.dtype)]
    rows += [wide(up_b), wide(mix_b), jnp.zeros((6, width), up_w.dtype)]
    return jnp.concatenate(rows, axis=0)


def shards(
    block_input, seq_lengths, project_weight, project_bias, dense_weight, up_weight, up_bias,
    down_weight, norm_gains, shift_vectors, cotangent,
):
    rows, _, own_count, width = block_input.shape
    n = lax.axis_size("tensor")
    places = lax.axis_size("ctx")
    extras = places - 1
    place = lax.axis_index("ctx")
    me = lax.axis_index("tensor")
    me1 = me.reshape(1)
    core1 = (lax.axis_index("dp") & 1).reshape(1)
    split = power_of_two()
    block_len = own_count * n
    tokens = rows * own_count
    heads = project_weight.shape[2] // (3 * HEAD_DIM)
    wide = heads * LANES
    k_rows = up_weight.shape[1]
    d_rows = dense_weight.shape[1]
    f_own = up_bias.shape[1]
    m_own = project_bias.shape[1]
    shard_count = lax.axis_size("dp") * places

    ends = jnp.cumsum(seq_lengths, axis=1)
    order = (me + jnp.arange(n, dtype=jnp.int32)) % n
    query_base = place * block_len + order * own_count
    slots = query_base[:, None] + jnp.arange(own_count, dtype=jnp.int32)[None]
    passed = (ends[:, None, None, :] <= slots[None, :, :, None]).astype(jnp.int32)
    begin = jnp.sum(passed * seq_lengths[:, None, None, :], axis=3)
    position = (slots[None] - begin).transpose(1, 0, 2).reshape(-1)
    frequency = 1.0 / 10000.0 ** (jnp.arange(0, ROTARY, 2, dtype=F32) / ROTARY)
    angle = frequency[:, None] * position.astype(F32)[None, :]
    cosine, sine = lax.optimization_barrier((jnp.cos(angle), jnp.sin(angle)))
    cosine, sine = cosine.T, sine.T
    ones = jnp.ones((cosine.shape[0], LANES - ROTARY), F32)
    zero8 = jnp.zeros_like(sine)
    tables = (
        jnp.concatenate([cosine, cosine, ones], axis=1).reshape(n, tokens, LANES),
        jnp.concatenate([-sine, zero8, ones * 0.0], axis=1).reshape(n, tokens, LANES),
        jnp.concatenate([zero8, sine, ones * 0.0], axis=1).reshape(n, tokens, LANES),
    )
    key_base = jnp.concatenate(
        [
            jnp.where(place >= e, (place - e) * block_len + order * own_count, FAR)
            for e in range(places)
        ]
    )
    base = jnp.concatenate([query_base, key_base])
    need = (key_base[None, None, :] <= query_base[None, :, None] + own_count - 1) & (
        key_base[None, None, :] + own_count - 1 >= begin[:, :, :1]
    )
    need = need.astype(jnp.int32)
    rank = jnp.cumsum(need, axis=2) - need
    blocks = key_base.shape[0]
    spot = jnp.arange(blocks, dtype=jnp.int32)
    chosen = (rank[..., None] == spot) & (need[..., None] > 0)
    listed = jnp.sum(chosen * spot[:, None], axis=2)
    need = jnp.concatenate([jnp.sum(need, axis=2, keepdims=True), listed], axis=2)
    need = need.astype(jnp.int32).reshape(rows, -1)
    begin = begin.reshape(rows, n, 1, own_count)

    gains = norm_gains.astype(F32)
    shifts = shift_vectors.astype(F32)
    packed = [
        pack_layer(
            project_weight[l], project_bias[l], dense_weight[l] if l else None, up_weight[l],
            up_bias[l], down_weight[l], heads,
        )
        for l in range(LAYERS)
    ]
    flat = lambda a: a.reshape(n * tokens, -1)
    by_row = lambda a: a.reshape(n, rows, own_count, -1)
    stack = lambda chunks: jnp.stack(chunks)
    shift_to = lambda v, c: lax.ppermute(v, "tensor", [(s, (s + c) % n) for s in range(n)])
    sent = block_input[:, 0].reshape(tokens, width)
    sent0 = sent
    residual = sent.astype(F32)
    cot = cotangent[:, 0].reshape(tokens, width)

    spare = jnp.zeros((-d_rows % 8, width), BF)
    chunks0 = z_gather(jnp.concatenate([sent, dense_weight[0], spare], axis=0))
    gather_all = lambda v: lax.all_gather(v, ("dp", "ctx"), axis=0, tiled=False)
    gathered = [gather_all(packed[0])]
    gather_z = lambda v: lax.all_gather(v, "tensor", axis=0, tiled=False)
    vecs = [
        jnp.concatenate([gains[l].T, shifts[l].T, jnp.zeros((2, width), F32)], axis=0)
        for l in range(LAYERS)
    ]

    def mix_groups(chunks, l):
        cut = (n + 1) // 2
        tables_of = tables
        xs, first, q, kv_a = mix_pass(
            tokens, chunks[:cut], 0, n, gathered[l], k_rows, m_own, vecs[l], tables_of, heads
        )
        groups = [kv_a]
        if cut < n:
            chunks = chunks[:cut] + list(after(tuple(chunks[cut:]), kv_a))
            xs, first, q, kv_b = mix_pass(
                tokens, chunks[cut:], cut, n, gathered[l], k_rows, m_own, vecs[l], tables_of, heads,
                (xs, first, q),
            )
            groups.append(kv_b)
        groups = [a.reshape(a.shape[0], rows, own_count, wide) for a in groups]
        kvs = [groups] + [
            [lax.ppermute(a, "ctx", [(s, s + e) for s in range(places - e)]) for a in groups]
            for e in range(1, places)
        ]
        return xs, first, by_row(q), kvs, chunks

    chunks0[0] = after(chunks0[0], packed[1], need, base, begin)
    xs0, first0, q0, kvs0, chunks0 = mix_groups(chunks0, 0)
    dense_all = jnp.stack([chunk[tokens : tokens + d_rows] for chunk in chunks0])
    dense_all = gather_all(dense_all)
    second0, active0, slope0, parts = feed_pass(xs0, gathered[0], k_rows, f_own, vecs[0])
    later = gather_all(after(packed[1], parts[0]))
    shares = z_scatter(parts)
    mixed0, ot0, lse0 = attend(need, base, begin, after(q0, parts[0]), kvs0, heads)
    sent_mixed = [after(mixed0[0], *shares)] + mixed0[1:]
    sent_mixed = [sent_mixed[0]] + [shift_to(after(mixed0[c], *shares), c) for c in range(1, n)]
    residual, sent = join(me1, sent_mixed, dense_all, shares, residual, vecs[0])

    chunks1 = z_gather(sent)
    gathered.append(after(later, sent))
    xs1, first1, q1, kvs1, _ = mix_groups(chunks1, 1)
    second1, active1, slope1, parts = feed_pass(xs1, gathered[1], k_rows, f_own, vecs[1])
    cots = gather_z(after(cot.astype(BF), kvs1[0][0]))
    mixed1, ot1, lse1 = attend(need, base, begin, after(q1, parts[0]), kvs1, heads)
    do1, branches = middle(me1, mixed1, gathered[1], k_rows, d_rows, parts, cots)
    shares = z_scatter(branches)
    dq1, dkv1, *send_back = attend_back(need, base, begin, q1, do1, lse1, ot1, kvs1, heads)

    def return_pairs(sends):
        return [
            lax.ppermute(sends[e - 1], "ctx", [(s, s - e) for s in range(e, places)])
            for e in range(1, places)
        ]

    scatter_all = lambda v: lax.psum_scatter(v, ("dp", "ctx"), scatter_dimension=0, tiled=True)[0]

    own_cols = width // (n * shard_count)

    def extra_rows(sums_a):
        bias = unmix_columns(sums_a[2, : 2 * wide], heads).reshape(shard_count, 1, -1)
        return jnp.pad(bias, ((0, 0), (0, 7), (0, width - m_own)))

    def feed_out(total):
        total = total.astype(F32)
        return total[:k_rows], total[-8, :f_own], total[k_rows:-8]

    def mix_out(total):
        total = total.astype(F32)
        return unmix_columns(total[:k_rows], heads), total[-8, :m_own], total[k_rows:-8]

    got1 = return_pairs(send_back)
    cots = after(cots, dq1)
    cots = [lax.dynamic_index_in_dim(cots, (me + c) % n, 0, keepdims=False) for c in range(n)]
    scaled1, sums_b1, feed_g1 = feed_back(
        core1, cots, xs1, slope1, second1, active1, gathered[1], k_rows, vecs[1], places, False
    )
    feed1 = scatter_all(feed_g1)
    shares[0] = after(shares[0], dq1)
    block_output = shares[0].astype(F32)
    for share in shares[1:]:
        block_output = block_output + share.astype(F32)
    block_output = block_output + residual + shifts[1, :, 2] + shifts[1, :, 3]
    scaled1 = after(scaled1, block_output)
    gp1, parts1, sums_a1, _ = exit_pass(
        me1, core1, dq1, dkv1, got1, tables, xs1, gathered[1], k_rows, vecs[1], scaled1, heads, places
    )
    parts1 = z_scatter(parts1)
    rows1 = extra_rows(sums_a1)
    (mix_g1,) = mix_back(core1, first1, gp1, mixed1, cots, rows1, places, False, 30)

    grad, grad_own, token_sum0, *pieces = turn(
        me1, parts1, cot, chunks1[0], dense_all, (mix_g1, feed1)
    )
    do0 = [pieces[0]] + [None] * (n - 1)
    for c in range(1, n):
        do0[n - c] = shift_to(pieces[c], c)
    mix1 = scatter_all(after(mix_g1, *do0))
    gs = z_gather(after(grad_own, *do0))
    dq0, dkv0, *send_back = attend_back(need, base, begin, q0, do0, lse0, ot0, kvs0, heads)
    got0 = return_pairs(send_back)
    scaled0, sums_b0, *feed_g0 = feed_back(
        core1, gs, xs0, slope0, second0, active0, gathered[0], k_rows, vecs[0], places, split,
        (dq0,),
    )
    gp0, (parts0,), sums_a0, mix_g0 = exit_pass(
        me1, core1, dq0, dkv0, got0, tables, xs0, gathered[0], k_rows, vecs[0], scaled0, heads,
        places, 2 if split else 1, [first0] + mixed0 + gs, (mix1,),
    )
    parts0 = [lax.psum_scatter(parts0, "tensor", scatter_dimension=0, tiled=True)[0]]
    small = [
        jnp.stack([sums_a0[0], sums_b0[0], sums_a0[1], sums_b0[1], token_sum0[0]]),
        jnp.stack([sums_a1[0], sums_b1[0], sums_a1[1], sums_b1[1], token_sum0[1]]),
    ]
    sums = jnp.concatenate(small, axis=0).reshape(LAYERS * 5, n, shard_count, own_cols)
    sums = sums.transpose(1, 2, 0, 3)
    if split:
        feed_g0 = after(tuple(feed_g0), gp0)
        up_sum, rest_sum = Scatter(tuple(feed_g0[:2]), False), Scatter(tuple(feed_g0[2:]), True)
        mix_sum = Scatter(mix_g0, False)
        small_sum = Scatter(sums, False, ("tensor", "dp", "ctx"), F32)
        streams = [small_sum, mix_sum, up_sum, rest_sum]
        while mix_sum.order:
            advance(streams)
        (input_grad,) = turn(me1, parts0, grad, sent0)
        advance(streams, input_grad)
        while small_sum.order:
            advance(streams)
        mix0 = mix_out(mix_sum.value)
        feed0 = jnp.concatenate([up_sum.value, rest_sum.value], axis=0)
        total = small_sum.value
    else:
        (input_grad,) = turn(me1, parts0, grad, sent0)
        mix0 = mix_out(scatter_all(mix_g0[0]))
        feed0 = scatter_all(feed_g0[0])
        total = lax.psum_scatter(sums, "tensor", scatter_dimension=0, tiled=False)
        total = scatter_all(total)
    total = total.reshape(LAYERS, 5, own_cols)
    mix1 = mix_out(mix1)
    weight_out = []
    for feed_s, mix_s in ((feed_out(feed0), mix0), (feed_out(feed1), mix1)):
        weight_out.append((mix_s[0], mix_s[1], mix_s[2], feed_s[0], feed_s[1], feed_s[2]))

    gains_out = total[:, :2].transpose(0, 2, 1)
    shifts_out = jnp.stack([total[:, 2], total[:, 3], total[:, 4], total[:, 4]], axis=-1)
    outs = [jnp.stack([weight_out[l][j] for l in range(LAYERS)]) for j in range(6)]
    shape = (rows, 1, own_count, width)
    return (block_output.reshape(shape), input_grad.reshape(shape), *outs, gains_out, shifts_out)


def solution(mesh):
    in_specs = (
        P("dp", "ctx", "tensor", None),
        P("dp", None),
        P(None, ("dp", "ctx"), "tensor"),
        P(None, ("tensor", "dp", "ctx")),
        P(None, ("tensor", "dp", "ctx"), None),
        P(None, ("dp", "ctx"), "tensor"),
        P(None, ("tensor", "dp", "ctx")),
        P(None, ("tensor", "dp", "ctx"), None),
        P(),
        P(),
        P("dp", "ctx", "tensor", None),
    )
    out_specs = (
        P("dp", "ctx", "tensor", None),
        P("dp", "ctx", "tensor", None),
        P(None, ("dp", "ctx"), "tensor"),
        P(None, ("tensor", "dp", "ctx")),
        P(None, ("tensor", "dp", "ctx"), None),
        P(None, ("dp", "ctx"), "tensor"),
        P(None, ("tensor", "dp", "ctx")),
        P(None, ("tensor", "dp", "ctx"), None),
        P(None, ("tensor", "dp", "ctx"), None),
        P(None, ("tensor", "dp", "ctx"), None),
    )
    return jax.shard_map(shards, mesh=mesh, in_specs=in_specs, out_specs=out_specs, check_vma=False)
```

profile of v0, /device:TPU:0, one launch (start us, length us, event | category | flops | bytes accessed | tf_op | source)
XLA Modules:
  0.0 432.3 jit_solution(3476626621748523560)
XLA Ops:
  12.3 4.1 collective-permute-start
  30.8 15.6 %collective-permute-done.2.refs_1_ = bf16[280,768]{1,0:T(8,128)(2,1)} collective-permute-done((bf16[280,768]{1,0:T(8,128)(2,1)S(1)}, bf16[280,768]{1,0:T(8,128)(2,1)}, u32[]{:S(2)}, u32[]{:S(2)}) %collective-permute-start.2) | collective-permute-done | bytes 430112 | tf_op jit(solution)/shard_map/ppermute | solution.py:44
  49.4 4.7 %mix_pass.4 = (bf16[4,256,768]{2,1,0:T(8,128)(2,1)}, bf16[4,256,768]{2,1,0:T(8,128)(2,1)}, bf16[4,256,384]{2,1,0:T(8,128)(2,1)}, bf16[2,256,384]{2,1,0:T(8,128)(2,1)}) custom-call(bf16[280,768]{1,0:T(8,128)(2,1)} %copy-done.12, bf16[280,768]{1,0:T(8,128)(2,1)} %collective-permute-done.2.refs_1_, bf16[8,296,768]{2,1,0:T(8,128)(2,1)} %bitcast.308, ...), custom_call_target="tpu_custom_call" | custom-call | flops 13200000000 | bytes 43200000 | tf_op jit(solution)/shard_map/mix_pass/pallas_call | solution.py:217
  59.0 4.8 %mix_pass.5 = (bf16[4,256,768]{2,1,0:T(8,128)(2,1)}, bf16[4,256,768]{2,1,0:T(8,128)(2,1)}, bf16[4,256,384]{2,1,0:T(8,128)(2,1)}, bf16[2,256,384]{2,1,0:T(8,128)(2,1)}) custom-call(bf16[280,768]{1,0:T(8,128)(2,1)} %copy-done.29, bf16[280,768]{1,0:T(8,128)(2,1)} %collective-permute-done.1.refs_1_, ...), custom_call_target="tpu_custom_call", output_to_operand_aliasing={{0}: (8, {}), {1}: (9, {}), {2}: (10, {})} | custom-call | flops 13200000000 | bytes 43200000 | tf_op jit(solution)/shard_map/mix_pass/pallas_call | solution.py:217
  65.1 9.0 %feed_pass.2 = (bf16[4,256,768]{2,1,0:T(8,128)(2,1)}, bf16[4,256,768]{2,1,0:T(8,128)(2,1)}, bf16[4,256,768]{2,1,0:T(8,128)(2,1)}, bf16[256,768]{1,0:T(8,128)(2,1...) custom-call(bf16[4,256,768]{2,1,0:T(8,128)(2,1)} %get-tuple-element.141.refs_0_.refs_4_, ...), custom_call_target="tpu_custom_call" | custom-call | flops 22000001024 | bytes 72000000 | tf_op jit(solution)/shard_map/feed_pass/pallas_call | solution.py:240
  74.1 6.1 %collective-permute-start.5 = (bf16[256,768]{1,0:T(8,128)(2,1)}, bf16[256,768]{1,0:T(8,128)(2,1)}, u32[]{:S(2)}, u32[]{:S(2)}) collective-permute-start(bf16[256,768]{1,0:T(8,128)(2,1)} %get-tuple-element.148), channel_id=1, source_target_pairs={{0,8},{8,16},{16,24},{24,0},{1,9},{9,17},{17,25},{25,1},{2,10},{10... | collective-permute-start | bytes 1179656 | tf_op jit(solution)/shard_map/ppermute | solution.py:51
  85.3 9.2 %attend.2 = (bf16[1,256,192]{2,1,0:T(8,128)(2,1)}, bf16[1,256,192]{2,1,0:T(8,128)(2,1)}, bf16[1,256,192]{2,1,0:T(8,128)(2,1)}, bf16[1,256,192]{2,1,0:T(8,128)(2,...) custom-call(s32[1,36]{1,0:T(1,128)} %reshape.657.need_ref, s32[12]{0:T(128)} %pad_add_fusion.2.base_ref, ...), custom_call_target="tpu_custom_call" | custom-call | flops 439999987712 | bytes 1440000000 | tf_op jit(solution)/shard_map/attend/pallas_call | solution.py:403
  94.5 9.8 %collective-permute-done.6.refs_6_ = bf16[256,768]{1,0:T(8,128)(2,1)} collective-permute-done((bf16[256,768]{1,0:T(8,128)(2,1)}, bf16[256,768]{1,0:T(8,128)(2,1)}, u32[]{:S(2)}, u32[]{:S(2)}) %collective-permute-start.6) | collective-permute-done | bytes 393248 | tf_op jit(solution)/shard_map/ppermute | solution.py:51
  104.7 8.9 %collective-permute-start.8 = (bf16[256,192]{1,0:T(8,128)(2,1)}, bf16[256,192]{1,0:T(8,128)(2,1)S(1)}, u32[]{:S(2)}, u32[]{:S(2)}) collective-permute-start(bf16[256,192]{1,0:T(8,128)(2,1)} %bitcast.338), channel_id=1, source_target_pairs={{0,8},{8,16},{16,24},{24,0},{1,9},{9,17},{17,25},{25,1},{2,10},{10... | collective-permute-start | bytes 294920 | tf_op jit(solution)/shard_map/ppermute | solution.py:1018
  135.6 7.0 %collective-permute-done.11.refs_1_ = bf16[256,768]{1,0:T(8,128)(2,1)S(1)} collective-permute-done((bf16[256,768]{1,0:T(8,128)(2,1)}, bf16[256,768]{1,0:T(8,128)(2,1)S(1)}, u32[]{:S(2)}, u32[]{:S(2)}) %collective-permute-start.11) | collective-permute-done | bytes 393248 | tf_op jit(solution)/shard_map/ppermute | solution.py:44
  143.3 4.7 %mix_pass.6 = (bf16[4,256,768]{2,1,0:T(8,128)(2,1)}, bf16[4,256,768]{2,1,0:T(8,128)(2,1)}, bf16[4,256,384]{2,1,0:T(8,128)(2,1)}, bf16[2,256,384]{2,1,0:T(8,128)(2,1)}) custom-call(bf16[256,768]{1,0:T(8,128)(2,1)} %get-tuple-element.158.refs_0_.refs_5_, bf16[256,768]{1,0:T(8,128)(2,1)} %copy-done.38, bf16[8,320,768]{2,1,0:T(8,128)(2,1)} %bitcast.297, ...), custom_call_target="tpu_custom_call" | custom-call | flops 13200000000 | bytes 43200000 | tf_op jit(solution)/shard_map/mix_pass/pallas_call | solution.py:217
  149.5 18.3 %collective-permute-done.12.refs_0_ = bf16[256,768]{1,0:T(8,128)(2,1)S(1)} collective-permute-done((bf16[256,768]{1,0:T(8,128)(2,1)}, bf16[256,768]{1,0:T(8,128)(2,1)S(1)}, u32[]{:S(2)}, u32[]{:S(2)}) %collective-permute-start.12) | collective-permute-done | bytes 393248 | tf_op jit(solution)/shard_map/ppermute | solution.py:44
  168.7 4.7 %mix_pass.7 = (bf16[4,256,768]{2,1,0:T(8,128)(2,1)}, bf16[4,256,768]{2,1,0:T(8,128)(2,1)}, bf16[4,256,384]{2,1,0:T(8,128)(2,1)}, bf16[2,256,384]{2,1,0:T(8,128)(2,1)}) custom-call(bf16[256,768]{1,0:T(8,128)(2,1)} %copy-done.48, bf16[256,768]{1,0:T(8,128)(2,1)} %copy-done.49, ...), custom_call_target="tpu_custom_call", output_to_operand_aliasing={{0}: (8, {}), {1}: (9, {}), {2}: (10, {})} | custom-call | flops 13200000000 | bytes 43200000 | tf_op jit(solution)/shard_map/mix_pass/pallas_call | solution.py:217
  175.5 9.0 %feed_pass.3 = (bf16[4,256,768]{2,1,0:T(8,128)(2,1)}, bf16[4,256,768]{2,1,0:T(8,128)(2,1)}, bf16[4,256,768]{2,1,0:T(8,128)(2,1)}, bf16[256,768]{1,0:T(8,128)(2,1...) custom-call(bf16[4,256,768]{2,1,0:T(8,128)(2,1)} %get-tuple-element.168.refs_0_.refs_4_, ...), custom_call_target="tpu_custom_call" | custom-call | flops 22000001024 | bytes 72000000 | tf_op jit(solution)/shard_map/feed_pass/pallas_call | solution.py:240
  185.9 9.2 %attend.3 = (bf16[1,256,192]{2,1,0:T(8,128)(2,1)}, bf16[1,256,192]{2,1,0:T(8,128)(2,1)}, bf16[1,256,192]{2,1,0:T(8,128)(2,1)}, bf16[1,256,192]{2,1,0:T(8,128)(2,...) custom-call(s32[1,36]{1,0:T(1,128)} %reshape.657.need_ref, s32[12]{0:T(128)} %pad_add_fusion.2.base_ref, ...), custom_call_target="tpu_custom_call" | custom-call | flops 439999987712 | bytes 1440000000 | tf_op jit(solution)/shard_map/attend/pallas_call | solution.py:403
  195.1 7.3 %all-gather.15.cloned.1.call-done = bf16[1024,768]{1,0:T(8,128)(2,1)} async-done(((bf16[256,768]{1,0:T(8,128)(2,1)}), bf16[1024,768]{1,0:T(8,128)(2,1)}) %all-gather.15.cloned.1.call-update) | async-done | bytes 1572880 | tf_op jit(solution)/shard_map/all_gather | solution.py:1028
  209.8 13.0 %attend_back.2 = (f32[4,1,256,384]{3,2,1,0:T(8,128)}, f32[4,1,256,384]{3,2,1,0:T(8,128)}, bf16[4,1,256,384]{3,2,1,0:T(8,128)(2,1)}) custom-call(s32[1,36]{1,0:T(1,128)} %reshape.657.need_ref, s32[12]{0:T(128)} %pad_add_fusion.2.base_ref, s32[1,4,1,256]{3,2,1,0:T(1,128)} %reshape.658.begin_ref, bf16[4,1,256,384]{3,2,1,0:T(8,128)(2,1)} %bitcast.355, ...), custom_call_target="tpu_custom_call" | custom-call | flops 44000002048 | bytes 144000000 | tf_op jit(solution)/shard_map/attend_back/pallas_call | solution.py:506
  225.5 11.1 %feed_back.2 = (f32[4,256,768]{2,1,0:T(8,128)}, f32[8,768]{1,0:T(8,128)}, bf16[8,200,768]{2,1,0:T(8,128)(2,1)}) custom-call(s32[1]{0:T(128)} %bitcast.67.core_ref, bf16[256,768]{1,0:T(8,128)(2,1)} %get-tuple-element.323.refs_0_.refs_7_, bf16[256,768]{1,0:T(8,128)(2,1)} %get-tuple-element.322.refs_1_.refs_8_, ...), custom_call_target="tpu_custom_call" | custom-call | flops 13200000000 | bytes 43200000 | tf_op jit(solution)/shard_map/feed_back/pallas_call | solution.py:622
  238.1 4.4 %collective-permute-done.17 = bf16[256,768]{1,0:T(8,128)(2,1)S(1)} collective-permute-done((bf16[256,768]{1,0:T(8,128)(2,1)}, bf16[256,768]{1,0:T(8,128)(2,1)S(1)}, u32[]{:S(2)}, u32[]{:S(2)}) %collective-permute-start.17) | collective-permute-done | bytes 393248 | tf_op jit(solution)/shard_map/ppermute | solution.py:51
  245.8 8.6 %exit_pass.2 = (bf16[4,256,768]{2,1,0:T(8,128)(2,1)}, f32[8,768]{1,0:T(8,128)}, bf16[256,768]{1,0:T(8,128)(2,1)}, bf16[256,768]{1,0:T(8,128)(2,1)}, bf16[256,768]{1,0:T(8,128)(2,1)}, /*index=5*/bf16[256,768]{1,0:T(8,128)(2,1)}) custom-call(s32[1]{0:T(128)} %bitcast.me_ref._, s32[1]{0:T(128)} %bitcast.67.core_ref, f32[4,256,384]{2,1,0:T(8,128)} %bitcast.347, ...), custom_call_target="tpu_custom_call" | custom-call | flops 109999996928 | bytes 360000000 | tf_op jit(solution)/shard_map/exit_pass/pallas_call | solution.py:889
  261.5 6.5 %mix_back.1.refs_7_ = bf16[8,128,768]{2,1,0:T(8,128)(2,1)} custom-call(s32[1]{0:T(128)} %bitcast.67.core_ref, bf16[4,256,768]{2,1,0:T(8,128)(2,1)} %get-tuple-element.204.refs_0_, bf16[4,256,768]{2,1,0:T(8,128)(2,1)} %get-tuple-element.205.refs_1_, f32[8,8,768]{2,1,0:T(8,128)} %pad.24.refs_2_, bf16[256,192]{1,0:T(8,128)(2,1)} %bitcast.359, ...), custom_call_target="tpu_custom_call" | custom-call | flops 32999999488 | bytes 108000000 | tf_op jit(solution)/shard_map/mix_back/pallas_call | solution.py:685
  268.6 13.2 %collective-permute-done.21.refs_2_ = bf16[256,768]{1,0:T(8,128)(2,1)S(1)} collective-permute-done((bf16[256,768]{1,0:T(8,128)(2,1)}, bf16[256,768]{1,0:T(8,128)(2,1)S(1)}, u32[]{:S(2)}, u32[]{:S(2)}) %collective-permute-start.21) | collective-permute-done | bytes 393248 | tf_op jit(solution)/shard_map/ppermute | solution.py:51
  281.9 6.1 %reduce-scatter.4.cloned.1.call-done = bf16[1,200,768]{2,1,0:T(8,128)(2,1)} async-done(((bf16[8,200,768]{2,1,0:T(8,128)(2,1)}), bf16[1,200,768]{2,1,0:T(8,128)(2,1)}) %reduce-scatter.4.cloned.1.call-update) | async-done | bytes 307216 | tf_op jit(solution)/shard_map/reduce_scatter | solution.py:1083
  288.0 4.1 turn.2
  292.1 5.9 %collective-permute-start.23 = (bf16[256,192]{1,0:T(8,128)(2,1)}, bf16[256,192]{1,0:T(8,128)(2,1)S(1)}, u32[]{:S(2)}, u32[]{:S(2)}) collective-permute-start(bf16[256,192]{1,0:T(8,128)(2,1)} %get-tuple-element.209), channel_id=1, source_target_pairs={{0,24},{8,0},{16,8},{24,16},{1,25},{9,1},{17,9},{25,17},{2,26},{10... | collective-permute-start | bytes 294920 | tf_op jit(solution)/shard_map/ppermute | solution.py:1018
  302.3 6.8 %collective-permute-done.24 = bf16[256,192]{1,0:T(8,128)(2,1)S(1)} collective-permute-done((bf16[256,192]{1,0:T(8,128)(2,1)}, bf16[256,192]{1,0:T(8,128)(2,1)S(1)}, u32[]{:S(2)}, u32[]{:S(2)}) %collective-permute-start.24) | collective-permute-done | bytes 98336 | tf_op jit(solution)/shard_map/ppermute | solution.py:1018
  312.8 12.8 %attend_back.3 = (f32[4,1,256,384]{3,2,1,0:T(8,128)}, f32[4,1,256,384]{3,2,1,0:T(8,128)}, bf16[4,1,256,384]{3,2,1,0:T(8,128)(2,1)}) custom-call(s32[1,36]{1,0:T(1,128)} %reshape.657.need_ref, s32[12]{0:T(128)} %pad_add_fusion.2.base_ref, s32[1,4,1,256]{3,2,1,0:T(1,128)} %reshape.658.begin_ref, bf16[4,1,256,384]{3,2,1,0:T(8,128)(2,1)} %bitcast.353, ...), custom_call_target="tpu_custom_call" | custom-call | flops 44000002048 | bytes 144000000 | tf_op jit(solution)/shard_map/attend_back/pallas_call | solution.py:506
  327.1 17.2 %collective-permute-done.28.refs_2_.refs_15_ = bf16[256,768]{1,0:T(8,128)(2,1)S(1)} collective-permute-done((bf16[256,768]{1,0:T(8,128)(2,1)S(1)}, bf16[256,768]{1,0:T(8,128)(2,1)S(1)}, u32[]{:S(2)}, u32[]{:S(2)}) %collective-permute-start.28) | collective-permute-done | bytes 393248 | tf_op jit(solution)/shard_map/ppermute | solution.py:44
  345.2 11.1 %feed_back.3 = (f32[4,256,768]{2,1,0:T(8,128)}, f32[8,768]{1,0:T(8,128)}, bf16[4,96,768]{2,1,0:T(8,128)(2,1)}, bf16[4,96,768]{2,1,0:T(8,128)(2,1)}, bf16[4,104,7...) custom-call(s32[1]{0:T(128)} %bitcast.67.core_ref, bf16[256,768]{1,0:T(8,128)(2,1)} %get-tuple-element.218.refs_0_.refs_13_, ...), custom_call_target="tpu_custom_call" | custom-call | flops 13200000000 | bytes 43200000 | tf_op jit(solution)/shard_map/feed_back/pallas_call | solution.py:622
  358.4 11.1 %exit_pass.3 = (bf16[4,256,768]{2,1,0:T(8,128)(2,1)}, f32[8,768]{1,0:T(8,128)}, bf16[4,256,768]{2,1,0:T(8,128)(2,1)}, bf16[4,128,768]{2,1,0:T(8,128)(2,1)}, bf16[4,128,768]{2,1,0:T(8,128)(2,1)}) custom-call(s32[1]{0:T(128)} %bitcast.me_ref._, s32[1]{0:T(128)} %bitcast.67.core_ref, f32[4,256,384]{2,1,0:T(8,128)} %bitcast.349, f32[4,256,384]{2,1,0:T(8,128)} %bitcast.350, ...), custom_call_target="tpu_custom_call" | custom-call | flops 109999996928 | bytes 360000000 | tf_op jit(solution)/shard_map/exit_pass/pallas_call | solution.py:889
  387.1 11.4 %collective-permute-done.36 = bf16[2,96,768]{2,1,0:T(8,128)(2,1)S(1)} collective-permute-done((bf16[2,96,768]{2,1,0:T(8,128)(2,1)S(1)}, bf16[2,96,768]{2,1,0:T(8,128)(2,1)S(1)}, u32[]{:S(2)}, u32[]{:S(2)}) %collective-permute-start.36) | collective-permute-done | bytes 294944 | tf_op jit(solution)/shard_map/ppermute | solution.py:70
  402.6 8.2 %collective-permute-done.39 = bf16[96,768]{1,0:T(8,128)(2,1)S(1)} collective-permute-done((bf16[96,768]{1,0:T(8,128)(2,1)S(1)}, bf16[96,768]{1,0:T(8,128)(2,1)S(1)}, u32[]{:S(2)}, u32[]{:S(2)}) %collective-permute-start.39) | collective-permute-done | bytes 147488 | tf_op jit(solution)/shard_map/ppermute | solution.py:70
  (368 shorter events, 132.6 us)
Async XLA Ops:
  7.2 42.2 %all-gather.9.cloned.1.call-start = ((), (), s32[]{:S(2)}) async-start(), calls=%async_computation.6 | async-start | bytes 4091904 | tf_op jit(solution)/shard_map/all_gather | solution.py:1026
  12.1 112.1 %all-gather.13.cloned.1.call-start = ((), (), s32[]{:S(2)}) async-start(), calls=%async_computation.8 | async-start | bytes 1327104 | tf_op jit(solution)/shard_map/all_gather | solution.py:1026
  12.3 41.8 %collective-permute-start = (bf16[280,768]{1,0:T(8,128)(2,1)S(1)}, bf16[280,768]{1,0:T(8,128)(2,1)S(1)}, u32[]{:S(2)}, u32[]{:S(2)}) collective-permute-start(bf16[280,768]{1,0:T(8,128)(2,1)S(1)} %pad_maximum_fusion.3.refs_0_), channel_id=1, source_target_pairs={{0,16},{8,24},{16,0},{24,8},{1,17},{9,25},{17,1},{25,9},{2,18},{10... | collective-permute-start | bytes 1290248 | tf_op jit(solution)/shard_map/ppermute | solution.py:44
  16.4 37.7 %collective-permute-start.1 = (bf16[280,768]{1,0:T(8,128)(2,1)S(1)}, bf16[280,768]{1,0:T(8,128)(2,1)}, u32[]{:S(2)}, u32[]{:S(2)}) collective-permute-start(bf16[280,768]{1,0:T(8,128)(2,1)S(1)} %pad_maximum_fusion.3.refs_0_), channel_id=1, source_target_pairs={{0,8},{8,16},{16,24},{24,0},{1,9},{9,17},{17,25},{25,1},{2,10},{10... | collective-permute-start | bytes 1290248 | tf_op jit(solution)/shard_map/ppermute | solution.py:44
  18.0 28.5 %collective-permute-start.2 = (bf16[280,768]{1,0:T(8,128)(2,1)S(1)}, bf16[280,768]{1,0:T(8,128)(2,1)}, u32[]{:S(2)}, u32[]{:S(2)}) collective-permute-start(bf16[280,768]{1,0:T(8,128)(2,1)S(1)} %pad_maximum_fusion.3.refs_0_), channel_id=1, source_target_pairs={{0,24},{8,0},{16,8},{24,16},{1,25},{9,1},{17,9},{25,17},{2,26},{10... | collective-permute-start | bytes 1290248 | tf_op jit(solution)/shard_map/ppermute | solution.py:44
  55.6 80.0 %all-gather.11.cloned.1.call-start = ((), (), s32[]{:S(2)}) async-start(), calls=%async_computation.7 | async-start | bytes 4423680 | tf_op jit(solution)/shard_map/all_gather | solution.py:1026
  55.6 28.2 %collective-permute-start.3 = (bf16[2,1,256,384]{3,2,1,0:T(8,128)(2,1)}, bf16[2,1,256,384]{3,2,1,0:T(8,128)(2,1)S(1)}, u32[]{:S(2)}, u32[]{:S(2)}) collective-permute-start(bf16[2,1,256,384]{3,2,1,0:T(8,128)(2,1)} %bitcast.325), channel_id=1, source_target_pairs={{0,1},{2,3},{4,5},{6,7},{8,9},{10,11},{12,13},{14,15},{16,17},{18,... | collective-permute-start | bytes 1179656 | tf_op jit(solution)/shard_map/ppermute | solution.py:1050
  63.8 20.0 %collective-permute-start.4 = (bf16[2,1,256,384]{3,2,1,0:T(8,128)(2,1)}, bf16[2,1,256,384]{3,2,1,0:T(8,128)(2,1)S(1)}, u32[]{:S(2)}, u32[]{:S(2)}) collective-permute-start(bf16[2,1,256,384]{3,2,1,0:T(8,128)(2,1)} %bitcast.328), channel_id=1, source_target_pairs={{0,1},{2,3},{4,5},{6,7},{8,9},{10,11},{12,13},{14,15},{16,17},{18,... | collective-permute-start | bytes 1179656 | tf_op jit(solution)/shard_map/ppermute | solution.py:1050
  74.1 20.4 %collective-permute-start.5 = (bf16[256,768]{1,0:T(8,128)(2,1)}, bf16[256,768]{1,0:T(8,128)(2,1)}, u32[]{:S(2)}, u32[]{:S(2)}) collective-permute-start(bf16[256,768]{1,0:T(8,128)(2,1)} %get-tuple-element.148), channel_id=1, source_target_pairs={{0,8},{8,16},{16,24},{24,0},{1,9},{9,17},{17,25},{25,1},{2,10},{10... | collective-permute-start | bytes 1179656 | tf_op jit(solution)/shard_map/ppermute | solution.py:51
  80.3 24.0 %collective-permute-start.6 = (bf16[256,768]{1,0:T(8,128)(2,1)}, bf16[256,768]{1,0:T(8,128)(2,1)}, u32[]{:S(2)}, u32[]{:S(2)}) collective-permute-start(bf16[256,768]{1,0:T(8,128)(2,1)} %get-tuple-element.149), channel_id=1, source_target_pairs={{0,16},{8,24},{16,0},{24,8},{1,17},{9,25},{17,1},{25,9},{2,18},{10... | collective-permute-start | bytes 1179656 | tf_op jit(solution)/shard_map/ppermute | solution.py:51
  80.3 24.5 %collective-permute-start.7 = (bf16[256,768]{1,0:T(8,128)(2,1)}, bf16[256,768]{1,0:T(8,128)(2,1)}, u32[]{:S(2)}, u32[]{:S(2)}) collective-permute-start(bf16[256,768]{1,0:T(8,128)(2,1)} %get-tuple-element.150), channel_id=1, source_target_pairs={{0,24},{8,0},{16,8},{24,16},{1,25},{9,1},{17,9},{25,17},{2,26},{10... | collective-permute-start | bytes 1179656 | tf_op jit(solution)/shard_map/ppermute | solution.py:51
  83.7 118.7 %all-gather.15.cloned.1.call-start = ((), (), s32[]{:S(2)}) async-start(), calls=%async_computation.9 | async-start | bytes 1966080 | tf_op jit(solution)/shard_map/all_gather | solution.py:1028
  104.7 16.4 %collective-permute-start.8 = (bf16[256,192]{1,0:T(8,128)(2,1)}, bf16[256,192]{1,0:T(8,128)(2,1)S(1)}, u32[]{:S(2)}, u32[]{:S(2)}) collective-permute-start(bf16[256,192]{1,0:T(8,128)(2,1)} %bitcast.338), channel_id=1, source_target_pairs={{0,8},{8,16},{16,24},{24,0},{1,9},{9,17},{17,25},{25,1},{2,10},{10... | collective-permute-start | bytes 294920 | tf_op jit(solution)/shard_map/ppermute | solution.py:1018
  134.8 33.0 %collective-permute-start.12 = (bf16[256,768]{1,0:T(8,128)(2,1)}, bf16[256,768]{1,0:T(8,128)(2,1)S(1)}, u32[]{:S(2)}, u32[]{:S(2)}) collective-permute-start(bf16[256,768]{1,0:T(8,128)(2,1)} %get-tuple-element.158.refs_0_.refs_5_), channel_id=1, source_target_pairs={{0,16},{8,24},{16,0},{24,8},{1,17},{9,25},{17,1},{25,9},{2,18},{10... | collective-permute-start | bytes 1179656 | tf_op jit(solution)/shard_map/ppermute | solution.py:44
  135.6 32.3 %collective-permute-start.13 = (bf16[256,768]{1,0:T(8,128)(2,1)}, bf16[256,768]{1,0:T(8,128)(2,1)S(1)}, u32[]{:S(2)}, u32[]{:S(2)}) collective-permute-start(bf16[256,768]{1,0:T(8,128)(2,1)} %get-tuple-element.158.refs_0_.refs_5_), channel_id=1, source_target_pairs={{0,8},{8,16},{16,24},{24,0},{1,9},{9,17},{17,25},{25,1},{2,10},{10... | collective-permute-start | bytes 1179656 | tf_op jit(solution)/shard_map/ppermute | solution.py:44
  148.0 36.4 %collective-permute-start.14 = (bf16[2,1,256,384]{3,2,1,0:T(8,128)(2,1)}, bf16[2,1,256,384]{3,2,1,0:T(8,128)(2,1)S(1)}, u32[]{:S(2)}, u32[]{:S(2)}) collective-permute-start(bf16[2,1,256,384]{3,2,1,0:T(8,128)(2,1)} %bitcast.332), channel_id=1, source_target_pairs={{0,1},{2,3},{4,5},{6,7},{8,9},{10,11},{12,13},{14,15},{16,17},{18,... | collective-permute-start | bytes 1179656 | tf_op jit(solution)/shard_map/ppermute | solution.py:1050
  149.5 138.5 %reduce-scatter.4.cloned.1.call-start = ((), (), s32[]{:S(2)}) async-start(), calls=%async_computation.3 | async-start | bytes 2764800 | tf_op jit(solution)/shard_map/reduce_scatter | solution.py:1083
  206.5 31.6 %collective-permute-start.18 = (bf16[256,768]{1,0:T(8,128)(2,1)}, bf16[256,768]{1,0:T(8,128)(2,1)S(1)}, u32[]{:S(2)}, u32[]{:S(2)}) collective-permute-start(bf16[256,768]{1,0:T(8,128)(2,1)} %get-tuple-element.190), channel_id=1, source_target_pairs={{0,24},{8,0},{16,8},{24,16},{1,25},{9,1},{17,9},{25,17},{2,26},{10... | collective-permute-start | bytes 1179656 | tf_op jit(solution)/shard_map/ppermute | solution.py:51
  207.7 34.8 %collective-permute-start.17 = (bf16[256,768]{1,0:T(8,128)(2,1)}, bf16[256,768]{1,0:T(8,128)(2,1)S(1)}, u32[]{:S(2)}, u32[]{:S(2)}) collective-permute-start(bf16[256,768]{1,0:T(8,128)(2,1)} %get-tuple-element.189), channel_id=1, source_target_pairs={{0,16},{8,24},{16,0},{24,8},{1,17},{9,25},{17,1},{25,9},{2,18},{10... | collective-permute-start | bytes 1179656 | tf_op jit(solution)/shard_map/ppermute | solution.py:51
  208.4 34.1 %collective-permute-start.16 = (bf16[256,768]{1,0:T(8,128)(2,1)}, bf16[256,768]{1,0:T(8,128)(2,1)S(1)}, u32[]{:S(2)}, u32[]{:S(2)}) collective-permute-start(bf16[256,768]{1,0:T(8,128)(2,1)} %get-tuple-element.188), channel_id=1, source_target_pairs={{0,8},{8,16},{16,24},{24,0},{1,9},{9,17},{17,25},{25,1},{2,10},{10... | collective-permute-start | bytes 1179656 | tf_op jit(solution)/shard_map/ppermute | solution.py:51
  222.8 22.2 %collective-permute-start.19 = (bf16[4,1,256,384]{3,2,0,1:T(8,128)(2,1)}, bf16[4,1,256,384]{3,2,0,1:T(8,128)(2,1)S(1)}, u32[]{:S(2)}, u32[]{:S(2)}) collective-permute-start(bf16[4,1,256,384]{3,2,0,1:T(8,128)(2,1)} %bitcast.320), channel_id=1, source_target_pairs={{1,0},{3,2},{5,4},{7,6},{9,8},{11,10},{13,12},{15,14},{17,16},{19,... | collective-permute-start | bytes 2359304 | tf_op jit(solution)/shard_map/ppermute | solution.py:1079
  236.6 121.7 %reduce-scatter.6.cloned.1.call-start = ((), (), s32[]{:S(2)}) async-start(), calls=%async_computation.4 | async-start | bytes 1769472 | tf_op jit(solution)/shard_map/reduce_scatter | solution.py:1083
  256.0 25.9 %collective-permute-start.21 = (bf16[256,768]{1,0:T(8,128)(2,1)}, bf16[256,768]{1,0:T(8,128)(2,1)S(1)}, u32[]{:S(2)}, u32[]{:S(2)}) collective-permute-start(bf16[256,768]{1,0:T(8,128)(2,1)} %get-tuple-element.202), channel_id=1, source_target_pairs={{0,16},{8,24},{16,0},{24,8},{1,17},{9,25},{17,1},{25,9},{2,18},{10... | collective-permute-start | bytes 1179656 | tf_op jit(solution)/shard_map/ppermute | solution.py:51
  257.5 24.4 %collective-permute-start.22 = (bf16[256,768]{1,0:T(8,128)(2,1)}, bf16[256,768]{1,0:T(8,128)(2,1)S(1)}, u32[]{:S(2)}, u32[]{:S(2)}) collective-permute-start(bf16[256,768]{1,0:T(8,128)(2,1)} %get-tuple-element.203), channel_id=1, source_target_pairs={{0,24},{8,0},{16,8},{24,16},{1,25},{9,1},{17,9},{25,17},{2,26},{10... | collective-permute-start | bytes 1179656 | tf_op jit(solution)/shard_map/ppermute | solution.py:51
  309.1 18.0 %collective-permute-start.27 = (bf16[256,768]{1,0:T(8,128)(2,1)S(1)}, bf16[256,768]{1,0:T(8,128)(2,1)S(1)}, u32[]{:S(2)}, u32[]{:S(2)}) collective-permute-start(bf16[256,768]{1,0:T(8,128)(2,1)S(1)} %copy-done.39), channel_id=1, source_target_pairs={{0,24},{8,0},{16,8},{24,16},{1,25},{9,1},{17,9},{25,17},{2,26},{10... | collective-permute-start | bytes 1179656 | tf_op jit(solution)/shard_map/ppermute | solution.py:44
  309.8 34.5 %collective-permute-start.28 = (bf16[256,768]{1,0:T(8,128)(2,1)S(1)}, bf16[256,768]{1,0:T(8,128)(2,1)S(1)}, u32[]{:S(2)}, u32[]{:S(2)}) collective-permute-start(bf16[256,768]{1,0:T(8,128)(2,1)S(1)} %copy-done.39), channel_id=1, source_target_pairs={{0,16},{8,24},{16,0},{24,8},{1,17},{9,25},{17,1},{25,9},{2,18},{10... | collective-permute-start | bytes 1179656 | tf_op jit(solution)/shard_map/ppermute | solution.py:44
  310.7 33.6 %collective-permute-start.29 = (bf16[256,768]{1,0:T(8,128)(2,1)S(1)}, bf16[256,768]{1,0:T(8,128)(2,1)S(1)}, u32[]{:S(2)}, u32[]{:S(2)}) collective-permute-start(bf16[256,768]{1,0:T(8,128)(2,1)S(1)} %copy-done.39), channel_id=1, source_target_pairs={{0,8},{8,16},{16,24},{24,0},{1,9},{9,17},{17,25},{25,1},{2,10},{10... | collective-permute-start | bytes 1179656 | tf_op jit(solution)/shard_map/ppermute | solution.py:44
  312.7 101.0 %reduce-scatter.8.cloned.1.call-start = ((), (), s32[]{:S(2)}) async-start(), calls=%async_computation.5 | async-start | bytes 1966080 | tf_op jit(solution)/shard_map/reduce_scatter | solution.py:1137
  325.6 31.6 %collective-permute-start.26 = (bf16[4,1,256,384]{3,2,0,1:T(8,128)(2,1)}, bf16[4,1,256,384]{3,2,0,1:T(8,128)(2,1)S(1)}, u32[]{:S(2)}, u32[]{:S(2)}) collective-permute-start(bf16[4,1,256,384]{3,2,0,1:T(8,128)(2,1)} %bitcast.323), channel_id=1, source_target_pairs={{1,0},{3,2},{5,4},{7,6},{9,8},{11,10},{13,12},{15,14},{17,16},{19,... | collective-permute-start | bytes 2359304 | tf_op jit(solution)/shard_map/ppermute | solution.py:1079
  381.0 17.7 %collective-permute-start.34 = (bf16[2,128,768]{2,1,0:T(8,128)(2,1)S(1)}, bf16[2,128,768]{2,1,0:T(8,128)(2,1)S(1)}, u32[]{:S(2)}, u32[]{:S(2)}) collective-permute-start(bf16[2,128,768]{2,1,0:T(8,128)(2,1)S(1)} %fusion), channel_id=1, source_target_pairs={{0,1},{1,0},{2,3},{3,2},{4,5},{5,4},{6,7},{7,6},{8,9},{9,8},{10,11... | collective-permute-start | bytes 1179656 | tf_op jit(solution)/shard_map/ppermute | solution.py:70
  382.5 16.0 %collective-permute-start.36 = (bf16[2,96,768]{2,1,0:T(8,128)(2,1)S(1)}, bf16[2,96,768]{2,1,0:T(8,128)(2,1)S(1)}, u32[]{:S(2)}, u32[]{:S(2)}) collective-permute-start(bf16[2,96,768]{2,1,0:T(8,128)(2,1)S(1)} %fusion.2), channel_id=1, source_target_pairs={{0,1},{1,0},{2,3},{3,2},{4,5},{5,4},{6,7},{7,6},{8,9},{9,8},{10,11... | collective-permute-start | bytes 884744 | tf_op jit(solution)/shard_map/ppermute | solution.py:70
  383.1 15.5 %collective-permute-start.37 = (bf16[2,104,768]{2,1,0:T(8,128)(2,1)S(1)}, bf16[2,104,768]{2,1,0:T(8,128)(2,1)S(1)}, u32[]{:S(2)}, u32[]{:S(2)}) collective-permute-start(bf16[2,104,768]{2,1,0:T(8,128)(2,1)S(1)} %fusion.1), channel_id=1, source_target_pairs={{0,4},{2,6},{4,0},{6,2},{1,5},{3,7},{5,1},{7,3},{8,12},{10,14},{12... | collective-permute-start | bytes 958472 | tf_op jit(solution)/shard_map/ppermute | solution.py:70
  (75 other events, 520.8 us)
Sparse Core Ops, SparseCore 0:
  12.3 37.0 all-gather.8
  55.7 29.4 all-gather.12
  87.6 35.7 all-gather.10
  149.6 52.7 all-gather.14
  236.7 51.2 reduce-scatter.3
  312.8 45.5 reduce-scatter.5
  372.6 37.5 reduce-scatter.7
where the time goes:
time: 441 us; the launch traced here: 432 us
  Pallas kernels  144 us (33%)
  waiting for transfers between devices  143 us (32%)
  starting transfers between devices  79.4 us (18%)
  local copies, waits for them, and re-layouts  33.9 us (8%)
  other arithmetic  16 us (4%)
  between operations  15.9 us (4%)
    ppermute x9, waiting for transfers between devices, z_gather(): lax.ppermute(own, 'tensor', [(s, (s - c) % n) for s in range(n)])  58.1 us
    ppermute x9, waiting for transfers between devices, z_scatter(): lax.ppermute(parts[c], 'tensor', [(s, (s + c) % n) for s in range(n)])  28.5 us
    pallas_call x2, Pallas kernels, attend_back(): pl.pallas_call(partial(attend_back_kernel, heads, extras, len(flat)), gri...  25.8 us
    ppermute x14, waiting for transfers between devices, flip(): lax.ppermute(send, axis, [(s, s ^ 1 << bit) for s in range(lax.axis_size(...  24.3 us
    pallas_call x2, Pallas kernels, feed_back(): pl.pallas_call(partial(feed_back_kernel, n, len(gates), inner, split), gr...  22.2 us
    pallas_call x2, Pallas kernels, exit_pass(): pl.pallas_call(partial(exit_kernel, n, heads, len(got), len(gates), inner...  19.7 us
    pallas_call x4, Pallas kernels, mix_pass(): pl.pallas_call(partial(mix_kernel, count, heads, own), grid=(count,), in_...  18.8 us
    ppermute x6, starting transfers between devices, shards(): lax.ppermute(v, 'tensor', [(s, (s + c) % n) for s in range(n)])  18.8 us
  transfers between devices with their start and end apart: 51, of which 25 were waited for; matrix products, arithmetic and copies ran while one was open for 8% of the time, Pallas kernels for 28%

commit v1 on v0

--- a/solution.py
+++ b/solution.py
@@ -1145,7 +1145,12 @@
         feed_g0 = after(tuple(feed_g0), gp0)
         up_sum, rest_sum = Scatter(tuple(feed_g0[:2]), False), Scatter(tuple(feed_g0[2:]), True)
         mix_sum = Scatter(mix_g0, False)
-        small_sum = Scatter(sums, False, ("tensor", "dp", "ctx"), F32)
+        picks = [lax.dynamic_index_in_dim(sums, (me + c) % n, 0, keepdims=False) for c in range(n)]
+        total = picks[0]
+        for c in range(1, n):
+            total = total + shift_to(picks[c], c)
+        advance([mix_sum, up_sum, rest_sum])
+        small_sum = Scatter(total, False, wire=F32)
         streams = [small_sum, mix_sum, up_sum, rest_sum]
         while mix_sum.order:
             advance(streams)

time: 441 us -> 442 us (level)
    ppermute x14 -> x12, starting transfers between devices: 16.5 us -> 7.32 us  [flip(): lax.ppermute(send, axis, [(s, s ^ 1 << bit) for s in range(lax.axis_size(...]
    ppermute x6 -> x9, starting transfers between devices: 18.8 us -> 27 us  [shards(): lax.ppermute(v, 'tensor', [(s, (s + c) % n) for s in range(n)])]
    reduce_scatter x2, waiting for transfers between devices: 7.34 us -> 0.02 us  [shards(): lax.psum_scatter(v, ('dp', 'ctx'), scatter_dimension=0, tiled=True)[0]]
    ppermute x2, waiting for transfers between devices: 1.27 us -> 8.45 us  [return_pairs(): lax.ppermute(sends[e - 1], 'ctx', [(s, s - e) for s in range(e, places)])]
    ppermute x6 -> x9, waiting for transfers between devices: 14 us -> 18.3 us  [shards(): lax.ppermute(v, 'tensor', [(s, (s + c) % n) for s in range(n)])]
    unnamed x126 -> x125, local copies, waits for them, and re-layouts: 11.7 us -> 13.4 us
    ppermute x14 -> x12, waiting for transfers between devices: 24.3 us -> 23.4 us  [flip(): lax.ppermute(send, axis, [(s, s ^ 1 << bit) for s in range(lax.axis_size(...]
  transfers between devices with their start and end apart: 51 -> 52, of which waited for: 25 -> 22; matrix products, arithmetic and copies ran while one was open for 8% -> 7% of each run, Pallas kernels for 28% -> 28%
where the time goes in v1:
time: 442 us; the launch traced here: 436 us
  waiting for transfers between devices  147 us (33%)
  Pallas kernels  144 us (33%)
  starting transfers between devices  77 us (17%)
  local copies, waits for them, and re-layouts  35.6 us (8%)
  other arithmetic  16 us (4%)
  between operations  15.9 us (4%)
    ppermute x9, waiting for transfers between devices, z_gather(): lax.ppermute(own, 'tensor', [(s, (s - c) % n) for s in range(n)])  57.9 us
    ppermute x9, waiting for transfers between devices, z_scatter(): lax.ppermute(parts[c], 'tensor', [(s, (s + c) % n) for s in range(n)])  29.6 us
    ppermute x9, starting transfers between devices, shards(): lax.ppermute(v, 'tensor', [(s, (s + c) % n) for s in range(n)])  27 us
    pallas_call x2, Pallas kernels, attend_back(): pl.pallas_call(partial(attend_back_kernel, heads, extras, len(flat)), gri...  25.8 us
    ppermute x12, waiting for transfers between devices, flip(): lax.ppermute(send, axis, [(s, s ^ 1 << bit) for s in range(lax.axis_size(...  23.4 us
    pallas_call x2, Pallas kernels, feed_back(): pl.pallas_call(partial(feed_back_kernel, n, len(gates), inner, split), gr...  22.2 us
    pallas_call x2, Pallas kernels, exit_pass(): pl.pallas_call(partial(exit_kernel, n, heads, len(got), len(gates), inner...  19.8 us
    pallas_call x4, Pallas kernels, mix_pass(): pl.pallas_call(partial(mix_kernel, count, heads, own), grid=(count,), in_...  18.8 us
  transfers between devices with their start and end apart: 52, of which 22 were waited for; matrix products, arithmetic and copies ran while one was open for 7% of the time, Pallas kernels for 28%

profile of v1, /device:TPU:0, one launch (start us, length us, event | category | flops | bytes accessed | tf_op | source)
XLA Modules:
  0.0 435.9 jit_solution(4389019168180897216)
XLA Ops:
  12.3 4.1 collective-permute-start
  30.8 15.6 %collective-permute-done.2.refs_1_ = bf16[280,768]{1,0:T(8,128)(2,1)} collective-permute-done((bf16[280,768]{1,0:T(8,128)(2,1)S(1)}, bf16[280,768]{1,0:T(8,128)(2,1)}, u32[]{:S(2)}, u32[]{:S(2)}) %collective-permute-start.2) | collective-permute-done | bytes 430112 | tf_op jit(solution)/shard_map/ppermute | solution.py:44
  49.4 4.7 %mix_pass.4 = (bf16[4,256,768]{2,1,0:T(8,128)(2,1)}, bf16[4,256,768]{2,1,0:T(8,128)(2,1)}, bf16[4,256,384]{2,1,0:T(8,128)(2,1)}, bf16[2,256,384]{2,1,0:T(8,128)(2,1)}) custom-call(bf16[280,768]{1,0:T(8,128)(2,1)} %copy-done.12, bf16[280,768]{1,0:T(8,128)(2,1)} %collective-permute-done.2.refs_1_, bf16[8,296,768]{2,1,0:T(8,128)(2,1)} %bitcast.324, ...), custom_call_target="tpu_custom_call" | custom-call | flops 13200000000 | bytes 43200000 | tf_op jit(solution)/shard_map/mix_pass/pallas_call | solution.py:217
  59.0 4.8 %mix_pass.5 = (bf16[4,256,768]{2,1,0:T(8,128)(2,1)}, bf16[4,256,768]{2,1,0:T(8,128)(2,1)}, bf16[4,256,384]{2,1,0:T(8,128)(2,1)}, bf16[2,256,384]{2,1,0:T(8,128)(2,1)}) custom-call(bf16[280,768]{1,0:T(8,128)(2,1)} %copy-done.29, bf16[280,768]{1,0:T(8,128)(2,1)} %collective-permute-done.1.refs_1_, ...), custom_call_target="tpu_custom_call", output_to_operand_aliasing={{0}: (8, {}), {1}: (9, {}), {2}: (10, {})} | custom-call | flops 13200000000 | bytes 43200000 | tf_op jit(solution)/shard_map/mix_pass/pallas_call | solution.py:217
  65.1 9.0 %feed_pass.2 = (bf16[4,256,768]{2,1,0:T(8,128)(2,1)}, bf16[4,256,768]{2,1,0:T(8,128)(2,1)}, bf16[4,256,768]{2,1,0:T(8,128)(2,1)}, bf16[256,768]{1,0:T(8,128)(2,1...) custom-call(bf16[4,256,768]{2,1,0:T(8,128)(2,1)} %get-tuple-element.140.refs_0_.refs_4_, ...), custom_call_target="tpu_custom_call" | custom-call | flops 22000001024 | bytes 72000000 | tf_op jit(solution)/shard_map/feed_pass/pallas_call | solution.py:240
  74.1 6.2 %collective-permute-start.5 = (bf16[256,768]{1,0:T(8,128)(2,1)}, bf16[256,768]{1,0:T(8,128)(2,1)}, u32[]{:S(2)}, u32[]{:S(2)}) collective-permute-start(bf16[256,768]{1,0:T(8,128)(2,1)} %get-tuple-element.147), channel_id=1, source_target_pairs={{0,8},{8,16},{16,24},{24,0},{1,9},{9,17},{17,25},{25,1},{2,10},{10... | collective-permute-start | bytes 1179656 | tf_op jit(solution)/shard_map/ppermute | solution.py:51
  85.3 9.2 %attend.2 = (bf16[1,256,192]{2,1,0:T(8,128)(2,1)}, bf16[1,256,192]{2,1,0:T(8,128)(2,1)}, bf16[1,256,192]{2,1,0:T(8,128)(2,1)}, bf16[1,256,192]{2,1,0:T(8,128)(2,...) custom-call(s32[1,36]{1,0:T(1,128)} %reshape.657.need_ref, s32[12]{0:T(128)} %pad_add_fusion.2.base_ref, ...), custom_call_target="tpu_custom_call" | custom-call | flops 439999987712 | bytes 1440000000 | tf_op jit(solution)/shard_map/attend/pallas_call | solution.py:403
  94.6 9.7 %collective-permute-done.6.refs_6_ = bf16[256,768]{1,0:T(8,128)(2,1)} collective-permute-done((bf16[256,768]{1,0:T(8,128)(2,1)}, bf16[256,768]{1,0:T(8,128)(2,1)}, u32[]{:S(2)}, u32[]{:S(2)}) %collective-permute-start.6) | collective-permute-done | bytes 393248 | tf_op jit(solution)/shard_map/ppermute | solution.py:51
  104.7 8.9 %collective-permute-start.8 = (bf16[256,192]{1,0:T(8,128)(2,1)}, bf16[256,192]{1,0:T(8,128)(2,1)S(1)}, u32[]{:S(2)}, u32[]{:S(2)}) collective-permute-start(bf16[256,192]{1,0:T(8,128)(2,1)} %bitcast.354), channel_id=1, source_target_pairs={{0,8},{8,16},{16,24},{24,0},{1,9},{9,17},{17,25},{25,1},{2,10},{10... | collective-permute-start | bytes 294920 | tf_op jit(solution)/shard_map/ppermute | solution.py:1018
  135.6 7.0 %collective-permute-done.11.refs_1_ = bf16[256,768]{1,0:T(8,128)(2,1)S(1)} collective-permute-done((bf16[256,768]{1,0:T(8,128)(2,1)}, bf16[256,768]{1,0:T(8,128)(2,1)S(1)}, u32[]{:S(2)}, u32[]{:S(2)}) %collective-permute-start.11) | collective-permute-done | bytes 393248 | tf_op jit(solution)/shard_map/ppermute | solution.py:44
  143.3 4.7 %mix_pass.6 = (bf16[4,256,768]{2,1,0:T(8,128)(2,1)}, bf16[4,256,768]{2,1,0:T(8,128)(2,1)}, bf16[4,256,384]{2,1,0:T(8,128)(2,1)}, bf16[2,256,384]{2,1,0:T(8,128)(2,1)}) custom-call(bf16[256,768]{1,0:T(8,128)(2,1)} %get-tuple-element.157.refs_0_.refs_5_, bf16[256,768]{1,0:T(8,128)(2,1)} %copy-done.38, bf16[8,320,768]{2,1,0:T(8,128)(2,1)} %bitcast.313, ...), custom_call_target="tpu_custom_call" | custom-call | flops 13200000000 | bytes 43200000 | tf_op jit(solution)/shard_map/mix_pass/pallas_call | solution.py:217
  149.5 18.3 %collective-permute-done.12.refs_0_ = bf16[256,768]{1,0:T(8,128)(2,1)S(1)} collective-permute-done((bf16[256,768]{1,0:T(8,128)(2,1)}, bf16[256,768]{1,0:T(8,128)(2,1)S(1)}, u32[]{:S(2)}, u32[]{:S(2)}) %collective-permute-start.12) | collective-permute-done | bytes 393248 | tf_op jit(solution)/shard_map/ppermute | solution.py:44
  168.7 4.7 %mix_pass.7 = (bf16[4,256,768]{2,1,0:T(8,128)(2,1)}, bf16[4,256,768]{2,1,0:T(8,128)(2,1)}, bf16[4,256,384]{2,1,0:T(8,128)(2,1)}, bf16[2,256,384]{2,1,0:T(8,128)(2,1)}) custom-call(bf16[256,768]{1,0:T(8,128)(2,1)} %copy-done.48, bf16[256,768]{1,0:T(8,128)(2,1)} %copy-done.49, ...), custom_call_target="tpu_custom_call", output_to_operand_aliasing={{0}: (8, {}), {1}: (9, {}), {2}: (10, {})} | custom-call | flops 13200000000 | bytes 43200000 | tf_op jit(solution)/shard_map/mix_pass/pallas_call | solution.py:217
  175.4 9.0 %feed_pass.3 = (bf16[4,256,768]{2,1,0:T(8,128)(2,1)}, bf16[4,256,768]{2,1,0:T(8,128)(2,1)}, bf16[4,256,768]{2,1,0:T(8,128)(2,1)}, bf16[256,768]{1,0:T(8,128)(2,1...) custom-call(bf16[4,256,768]{2,1,0:T(8,128)(2,1)} %get-tuple-element.167.refs_0_.refs_4_, ...), custom_call_target="tpu_custom_call" | custom-call | flops 22000001024 | bytes 72000000 | tf_op jit(solution)/shard_map/feed_pass/pallas_call | solution.py:240
  185.9 9.2 %attend.3 = (bf16[1,256,192]{2,1,0:T(8,128)(2,1)}, bf16[1,256,192]{2,1,0:T(8,128)(2,1)}, bf16[1,256,192]{2,1,0:T(8,128)(2,1)}, bf16[1,256,192]{2,1,0:T(8,128)(2,...) custom-call(s32[1,36]{1,0:T(1,128)} %reshape.657.need_ref, s32[12]{0:T(128)} %pad_add_fusion.2.base_ref, ...), custom_call_target="tpu_custom_call" | custom-call | flops 439999987712 | bytes 1440000000 | tf_op jit(solution)/shard_map/attend/pallas_call | solution.py:403
  195.1 7.2 %all-gather.15.cloned.1.call-done = bf16[1024,768]{1,0:T(8,128)(2,1)} async-done(((bf16[256,768]{1,0:T(8,128)(2,1)}), bf16[1024,768]{1,0:T(8,128)(2,1)}) %all-gather.15.cloned.1.call-update) | async-done | bytes 1572880 | tf_op jit(solution)/shard_map/all_gather | solution.py:1028
  209.6 13.0 %attend_back.2 = (f32[4,1,256,384]{3,2,1,0:T(8,128)}, f32[4,1,256,384]{3,2,1,0:T(8,128)}, bf16[4,1,256,384]{3,2,1,0:T(8,128)(2,1)}) custom-call(s32[1,36]{1,0:T(1,128)} %reshape.657.need_ref, s32[12]{0:T(128)} %pad_add_fusion.2.base_ref, s32[1,4,1,256]{3,2,1,0:T(1,128)} %reshape.658.begin_ref, bf16[4,1,256,384]{3,2,1,0:T(8,128)(2,1)} %bitcast.371, ...), custom_call_target="tpu_custom_call" | custom-call | flops 44000002048 | bytes 144000000 | tf_op jit(solution)/shard_map/attend_back/pallas_call | solution.py:506
  225.3 11.1 %feed_back.2 = (f32[4,256,768]{2,1,0:T(8,128)}, f32[8,768]{1,0:T(8,128)}, bf16[8,200,768]{2,1,0:T(8,128)(2,1)}) custom-call(s32[1]{0:T(128)} %bitcast.67.core_ref, bf16[256,768]{1,0:T(8,128)(2,1)} %get-tuple-element.321.refs_0_.refs_7_, bf16[256,768]{1,0:T(8,128)(2,1)} %get-tuple-element.320.refs_1_.refs_8_, ...), custom_call_target="tpu_custom_call" | custom-call | flops 13200000000 | bytes 43200000 | tf_op jit(solution)/shard_map/feed_back/pallas_call | solution.py:622
  238.0 4.4 %collective-permute-done.17 = bf16[256,768]{1,0:T(8,128)(2,1)S(1)} collective-permute-done((bf16[256,768]{1,0:T(8,128)(2,1)}, bf16[256,768]{1,0:T(8,128)(2,1)S(1)}, u32[]{:S(2)}, u32[]{:S(2)}) %collective-permute-start.17) | collective-permute-done | bytes 393248 | tf_op jit(solution)/shard_map/ppermute | solution.py:51
  243.5 8.0 %collective-permute-done.19 = bf16[4,1,256,384]{3,2,0,1:T(8,128)(2,1)S(1)} collective-permute-done((bf16[4,1,256,384]{3,2,0,1:T(8,128)(2,1)}, bf16[4,1,256,384]{3,2,0,1:T(8,128)(2,1)S(1)}, u32[]{:S(2)}, u32[]{:S(2)}) %collective-permute-start.19) | collective-permute-done | bytes 786464 | tf_op jit(solution)/shard_map/ppermute | solution.py:1079
  252.4 8.8 %exit_pass.2 = (bf16[4,256,768]{2,1,0:T(8,128)(2,1)}, f32[8,768]{1,0:T(8,128)}, bf16[256,768]{1,0:T(8,128)(2,1)}, bf16[256,768]{1,0:T(8,128)(2,1)}, bf16[256,768]{1,0:T(8,128)(2,1)}, /*index=5*/bf16[256,768]{1,0:T(8,128)(2,1)}) custom-call(s32[1]{0:T(128)} %bitcast.me_ref._, s32[1]{0:T(128)} %bitcast.67.core_ref, f32[4,256,384]{2,1,0:T(8,128)} %bitcast.363, ...), custom_call_target="tpu_custom_call" | custom-call | flops 109999996928 | bytes 360000000 | tf_op jit(solution)/shard_map/exit_pass/pallas_call | solution.py:889
  268.2 6.5 %mix_back.1.refs_7_ = bf16[8,128,768]{2,1,0:T(8,128)(2,1)} custom-call(s32[1]{0:T(128)} %bitcast.67.core_ref, bf16[4,256,768]{2,1,0:T(8,128)(2,1)} %get-tuple-element.203.refs_0_, bf16[4,256,768]{2,1,0:T(8,128)(2,1)} %get-tuple-element.204.refs_1_, f32[8,8,768]{2,1,0:T(8,128)} %pad.24.refs_2_, bf16[256,192]{1,0:T(8,128)(2,1)} %bitcast.375, ...), custom_call_target="tpu_custom_call" | custom-call | flops 32999999488 | bytes 108000000 | tf_op jit(solution)/shard_map/mix_back/pallas_call | solution.py:685
  275.4 14.3 %collective-permute-done.21.refs_2_ = bf16[256,768]{1,0:T(8,128)(2,1)S(1)} collective-permute-done((bf16[256,768]{1,0:T(8,128)(2,1)}, bf16[256,768]{1,0:T(8,128)(2,1)S(1)}, u32[]{:S(2)}, u32[]{:S(2)}) %collective-permute-start.21) | collective-permute-done | bytes 393248 | tf_op jit(solution)/shard_map/ppermute | solution.py:51
  290.6 4.1 turn.2
  294.7 8.9 %collective-permute-start.23 = (bf16[256,192]{1,0:T(8,128)(2,1)}, bf16[256,192]{1,0:T(8,128)(2,1)S(1)}, u32[]{:S(2)}, u32[]{:S(2)}) collective-permute-start(bf16[256,192]{1,0:T(8,128)(2,1)} %get-tuple-element.208), channel_id=1, source_target_pairs={{0,24},{8,0},{16,8},{24,16},{1,25},{9,1},{17,9},{25,17},{2,26},{10... | collective-permute-start | bytes 294920 | tf_op jit(solution)/shard_map/ppermute | solution.py:1018
  307.7 9.4 %collective-permute-done.24 = bf16[256,192]{1,0:T(8,128)(2,1)S(1)} collective-permute-done((bf16[256,192]{1,0:T(8,128)(2,1)}, bf16[256,192]{1,0:T(8,128)(2,1)S(1)}, u32[]{:S(2)}, u32[]{:S(2)}) %collective-permute-start.24) | collective-permute-done | bytes 98336 | tf_op jit(solution)/shard_map/ppermute | solution.py:1018
  319.3 12.8 %attend_back.3 = (f32[4,1,256,384]{3,2,1,0:T(8,128)}, f32[4,1,256,384]{3,2,1,0:T(8,128)}, bf16[4,1,256,384]{3,2,1,0:T(8,128)(2,1)}) custom-call(s32[1,36]{1,0:T(1,128)} %reshape.657.need_ref, s32[12]{0:T(128)} %pad_add_fusion.2.base_ref, s32[1,4,1,256]{3,2,1,0:T(1,128)} %reshape.658.begin_ref, bf16[4,1,256,384]{3,2,1,0:T(8,128)(2,1)} %bitcast.369, ...), custom_call_target="tpu_custom_call" | custom-call | flops 44000002048 | bytes 144000000 | tf_op jit(solution)/shard_map/attend_back/pallas_call | solution.py:506
  333.7 16.9 %collective-permute-done.28.refs_2_.refs_15_ = bf16[256,768]{1,0:T(8,128)(2,1)S(1)} collective-permute-done((bf16[256,768]{1,0:T(8,128)(2,1)S(1)}, bf16[256,768]{1,0:T(8,128)(2,1)S(1)}, u32[]{:S(2)}, u32[]{:S(2)}) %collective-permute-start.28) | collective-permute-done | bytes 393248 | tf_op jit(solution)/shard_map/ppermute | solution.py:44
  351.5 11.1 %feed_back.3 = (f32[4,256,768]{2,1,0:T(8,128)}, f32[8,768]{1,0:T(8,128)}, bf16[4,96,768]{2,1,0:T(8,128)(2,1)}, bf16[4,96,768]{2,1,0:T(8,128)(2,1)}, bf16[4,104,7...) custom-call(s32[1]{0:T(128)} %bitcast.67.core_ref, bf16[256,768]{1,0:T(8,128)(2,1)} %get-tuple-element.217.refs_0_.refs_13_, ...), custom_call_target="tpu_custom_call" | custom-call | flops 13200000000 | bytes 43200000 | tf_op jit(solution)/shard_map/feed_back/pallas_call | solution.py:622
  364.8 11.1 %exit_pass.3 = (bf16[4,256,768]{2,1,0:T(8,128)(2,1)}, f32[8,768]{1,0:T(8,128)}, bf16[4,256,768]{2,1,0:T(8,128)(2,1)}, bf16[4,128,768]{2,1,0:T(8,128)(2,1)}, bf16[4,128,768]{2,1,0:T(8,128)(2,1)}) custom-call(s32[1]{0:T(128)} %bitcast.me_ref._, s32[1]{0:T(128)} %bitcast.67.core_ref, f32[4,256,384]{2,1,0:T(8,128)} %bitcast.365, f32[4,256,384]{2,1,0:T(8,128)} %bitcast.366, ...), custom_call_target="tpu_custom_call" | custom-call | flops 109999996928 | bytes 360000000 | tf_op jit(solution)/shard_map/exit_pass/pallas_call | solution.py:889
  391.2 15.8 %collective-permute-done.38 = bf16[2,96,768]{2,1,0:T(8,128)(2,1)S(1)} collective-permute-done((bf16[2,96,768]{2,1,0:T(8,128)(2,1)S(1)}, bf16[2,96,768]{2,1,0:T(8,128)(2,1)S(1)}, u32[]{:S(2)}, u32[]{:S(2)}) %collective-permute-start.38) | collective-permute-done | bytes 294944 | tf_op jit(solution)/shard_map/ppermute | solution.py:70
  411.7 5.9 %collective-permute-done.41 = bf16[96,768]{1,0:T(8,128)(2,1)S(1)} collective-permute-done((bf16[96,768]{1,0:T(8,128)(2,1)S(1)}, bf16[96,768]{1,0:T(8,128)(2,1)S(1)}, u32[]{:S(2)}, u32[]{:S(2)}) %collective-permute-start.41) | collective-permute-done | bytes 147488 | tf_op jit(solution)/shard_map/ppermute | solution.py:70
  (368 shorter events, 125.9 us)
Async XLA Ops:
  7.2 42.2 %all-gather.9.cloned.1.call-start = ((), (), s32[]{:S(2)}) async-start(), calls=%async_computation.6 | async-start | bytes 4091904 | tf_op jit(solution)/shard_map/all_gather | solution.py:1026
  12.1 112.1 %all-gather.13.cloned.1.call-start = ((), (), s32[]{:S(2)}) async-start(), calls=%async_computation.8 | async-start | bytes 1327104 | tf_op jit(solution)/shard_map/all_gather | solution.py:1026
  12.3 41.7 %collective-permute-start = (bf16[280,768]{1,0:T(8,128)(2,1)S(1)}, bf16[280,768]{1,0:T(8,128)(2,1)S(1)}, u32[]{:S(2)}, u32[]{:S(2)}) collective-permute-start(bf16[280,768]{1,0:T(8,128)(2,1)S(1)} %pad_maximum_fusion.3.refs_0_), channel_id=1, source_target_pairs={{0,16},{8,24},{16,0},{24,8},{1,17},{9,25},{17,1},{25,9},{2,18},{10... | collective-permute-start | bytes 1290248 | tf_op jit(solution)/shard_map/ppermute | solution.py:44
  16.4 37.7 %collective-permute-start.1 = (bf16[280,768]{1,0:T(8,128)(2,1)S(1)}, bf16[280,768]{1,0:T(8,128)(2,1)}, u32[]{:S(2)}, u32[]{:S(2)}) collective-permute-start(bf16[280,768]{1,0:T(8,128)(2,1)S(1)} %pad_maximum_fusion.3.refs_0_), channel_id=1, source_target_pairs={{0,8},{8,16},{16,24},{24,0},{1,9},{9,17},{17,25},{25,1},{2,10},{10... | collective-permute-start | bytes 1290248 | tf_op jit(solution)/shard_map/ppermute | solution.py:44
  18.0 28.5 %collective-permute-start.2 = (bf16[280,768]{1,0:T(8,128)(2,1)S(1)}, bf16[280,768]{1,0:T(8,128)(2,1)}, u32[]{:S(2)}, u32[]{:S(2)}) collective-permute-start(bf16[280,768]{1,0:T(8,128)(2,1)S(1)} %pad_maximum_fusion.3.refs_0_), channel_id=1, source_target_pairs={{0,24},{8,0},{16,8},{24,16},{1,25},{9,1},{17,9},{25,17},{2,26},{10... | collective-permute-start | bytes 1290248 | tf_op jit(solution)/shard_map/ppermute | solution.py:44
  55.6 80.0 %all-gather.11.cloned.1.call-start = ((), (), s32[]{:S(2)}) async-start(), calls=%async_computation.7 | async-start | bytes 4423680 | tf_op jit(solution)/shard_map/all_gather | solution.py:1026
  55.6 28.2 %collective-permute-start.3 = (bf16[2,1,256,384]{3,2,1,0:T(8,128)(2,1)}, bf16[2,1,256,384]{3,2,1,0:T(8,128)(2,1)S(1)}, u32[]{:S(2)}, u32[]{:S(2)}) collective-permute-start(bf16[2,1,256,384]{3,2,1,0:T(8,128)(2,1)} %bitcast.341), channel_id=1, source_target_pairs={{0,1},{2,3},{4,5},{6,7},{8,9},{10,11},{12,13},{14,15},{16,17},{18,... | collective-permute-start | bytes 1179656 | tf_op jit(solution)/shard_map/ppermute | solution.py:1050
  63.8 20.0 %collective-permute-start.4 = (bf16[2,1,256,384]{3,2,1,0:T(8,128)(2,1)}, bf16[2,1,256,384]{3,2,1,0:T(8,128)(2,1)S(1)}, u32[]{:S(2)}, u32[]{:S(2)}) collective-permute-start(bf16[2,1,256,384]{3,2,1,0:T(8,128)(2,1)} %bitcast.344), channel_id=1, source_target_pairs={{0,1},{2,3},{4,5},{6,7},{8,9},{10,11},{12,13},{14,15},{16,17},{18,... | collective-permute-start | bytes 1179656 | tf_op jit(solution)/shard_map/ppermute | solution.py:1050
  74.1 20.4 %collective-permute-start.5 = (bf16[256,768]{1,0:T(8,128)(2,1)}, bf16[256,768]{1,0:T(8,128)(2,1)}, u32[]{:S(2)}, u32[]{:S(2)}) collective-permute-start(bf16[256,768]{1,0:T(8,128)(2,1)} %get-tuple-element.147), channel_id=1, source_target_pairs={{0,8},{8,16},{16,24},{24,0},{1,9},{9,17},{17,25},{25,1},{2,10},{10... | collective-permute-start | bytes 1179656 | tf_op jit(solution)/shard_map/ppermute | solution.py:51
  80.3 24.0 %collective-permute-start.6 = (bf16[256,768]{1,0:T(8,128)(2,1)}, bf16[256,768]{1,0:T(8,128)(2,1)}, u32[]{:S(2)}, u32[]{:S(2)}) collective-permute-start(bf16[256,768]{1,0:T(8,128)(2,1)} %get-tuple-element.148), channel_id=1, source_target_pairs={{0,16},{8,24},{16,0},{24,8},{1,17},{9,25},{17,1},{25,9},{2,18},{10... | collective-permute-start | bytes 1179656 | tf_op jit(solution)/shard_map/ppermute | solution.py:51
  80.3 24.5 %collective-permute-start.7 = (bf16[256,768]{1,0:T(8,128)(2,1)}, bf16[256,768]{1,0:T(8,128)(2,1)}, u32[]{:S(2)}, u32[]{:S(2)}) collective-permute-start(bf16[256,768]{1,0:T(8,128)(2,1)} %get-tuple-element.149), channel_id=1, source_target_pairs={{0,24},{8,0},{16,8},{24,16},{1,25},{9,1},{17,9},{25,17},{2,26},{10... | collective-permute-start | bytes 1179656 | tf_op jit(solution)/shard_map/ppermute | solution.py:51
  83.8 118.5 %all-gather.15.cloned.1.call-start = ((), (), s32[]{:S(2)}) async-start(), calls=%async_computation.9 | async-start | bytes 1966080 | tf_op jit(solution)/shard_map/all_gather | solution.py:1028
  104.7 16.4 %collective-permute-start.8 = (bf16[256,192]{1,0:T(8,128)(2,1)}, bf16[256,192]{1,0:T(8,128)(2,1)S(1)}, u32[]{:S(2)}, u32[]{:S(2)}) collective-permute-start(bf16[256,192]{1,0:T(8,128)(2,1)} %bitcast.354), channel_id=1, source_target_pairs={{0,8},{8,16},{16,24},{24,0},{1,9},{9,17},{17,25},{25,1},{2,10},{10... | collective-permute-start | bytes 294920 | tf_op jit(solution)/shard_map/ppermute | solution.py:1018
  134.8 33.0 %collective-permute-start.12 = (bf16[256,768]{1,0:T(8,128)(2,1)}, bf16[256,768]{1,0:T(8,128)(2,1)S(1)}, u32[]{:S(2)}, u32[]{:S(2)}) collective-permute-start(bf16[256,768]{1,0:T(8,128)(2,1)} %get-tuple-element.157.refs_0_.refs_5_), channel_id=1, source_target_pairs={{0,16},{8,24},{16,0},{24,8},{1,17},{9,25},{17,1},{25,9},{2,18},{10... | collective-permute-start | bytes 1179656 | tf_op jit(solution)/shard_map/ppermute | solution.py:44
  135.6 32.2 %collective-permute-start.13 = (bf16[256,768]{1,0:T(8,128)(2,1)}, bf16[256,768]{1,0:T(8,128)(2,1)S(1)}, u32[]{:S(2)}, u32[]{:S(2)}) collective-permute-start(bf16[256,768]{1,0:T(8,128)(2,1)} %get-tuple-element.157.refs_0_.refs_5_), channel_id=1, source_target_pairs={{0,8},{8,16},{16,24},{24,0},{1,9},{9,17},{17,25},{25,1},{2,10},{10... | collective-permute-start | bytes 1179656 | tf_op jit(solution)/shard_map/ppermute | solution.py:44
  148.0 36.4 %collective-permute-start.14 = (bf16[2,1,256,384]{3,2,1,0:T(8,128)(2,1)}, bf16[2,1,256,384]{3,2,1,0:T(8,128)(2,1)S(1)}, u32[]{:S(2)}, u32[]{:S(2)}) collective-permute-start(bf16[2,1,256,384]{3,2,1,0:T(8,128)(2,1)} %bitcast.348), channel_id=1, source_target_pairs={{0,1},{2,3},{4,5},{6,7},{8,9},{10,11},{12,13},{14,15},{16,17},{18,... | collective-permute-start | bytes 1179656 | tf_op jit(solution)/shard_map/ppermute | solution.py:1050
  149.5 140.2 %reduce-scatter.4.cloned.1.call-start = ((), (), s32[]{:S(2)}) async-start(), calls=%async_computation.3 | async-start | bytes 2764800 | tf_op jit(solution)/shard_map/reduce_scatter | solution.py:1083
  206.3 31.6 %collective-permute-start.18 = (bf16[256,768]{1,0:T(8,128)(2,1)}, bf16[256,768]{1,0:T(8,128)(2,1)S(1)}, u32[]{:S(2)}, u32[]{:S(2)}) collective-permute-start(bf16[256,768]{1,0:T(8,128)(2,1)} %get-tuple-element.189), channel_id=1, source_target_pairs={{0,24},{8,0},{16,8},{24,16},{1,25},{9,1},{17,9},{25,17},{2,26},{10... | collective-permute-start | bytes 1179656 | tf_op jit(solution)/shard_map/ppermute | solution.py:51
  207.6 34.8 %collective-permute-start.17 = (bf16[256,768]{1,0:T(8,128)(2,1)}, bf16[256,768]{1,0:T(8,128)(2,1)S(1)}, u32[]{:S(2)}, u32[]{:S(2)}) collective-permute-start(bf16[256,768]{1,0:T(8,128)(2,1)} %get-tuple-element.188), channel_id=1, source_target_pairs={{0,16},{8,24},{16,0},{24,8},{1,17},{9,25},{17,1},{25,9},{2,18},{10... | collective-permute-start | bytes 1179656 | tf_op jit(solution)/shard_map/ppermute | solution.py:51
  208.3 34.1 %collective-permute-start.16 = (bf16[256,768]{1,0:T(8,128)(2,1)}, bf16[256,768]{1,0:T(8,128)(2,1)S(1)}, u32[]{:S(2)}, u32[]{:S(2)}) collective-permute-start(bf16[256,768]{1,0:T(8,128)(2,1)} %get-tuple-element.187), channel_id=1, source_target_pairs={{0,8},{8,16},{16,24},{24,0},{1,9},{9,17},{17,25},{25,1},{2,10},{10... | collective-permute-start | bytes 1179656 | tf_op jit(solution)/shard_map/ppermute | solution.py:51
  222.6 28.9 %collective-permute-start.19 = (bf16[4,1,256,384]{3,2,0,1:T(8,128)(2,1)}, bf16[4,1,256,384]{3,2,0,1:T(8,128)(2,1)S(1)}, u32[]{:S(2)}, u32[]{:S(2)}) collective-permute-start(bf16[4,1,256,384]{3,2,0,1:T(8,128)(2,1)} %bitcast.336), channel_id=1, source_target_pairs={{1,0},{3,2},{5,4},{7,6},{9,8},{11,10},{13,12},{15,14},{17,16},{19,... | collective-permute-start | bytes 2359304 | tf_op jit(solution)/shard_map/ppermute | solution.py:1079
  236.5 127.4 %reduce-scatter.6.cloned.1.call-start = ((), (), s32[]{:S(2)}) async-start(), calls=%async_computation.4 | async-start | bytes 1769472 | tf_op jit(solution)/shard_map/reduce_scatter | solution.py:1083
  262.8 26.9 %collective-permute-start.21 = (bf16[256,768]{1,0:T(8,128)(2,1)}, bf16[256,768]{1,0:T(8,128)(2,1)S(1)}, u32[]{:S(2)}, u32[]{:S(2)}) collective-permute-start(bf16[256,768]{1,0:T(8,128)(2,1)} %get-tuple-element.201), channel_id=1, source_target_pairs={{0,16},{8,24},{16,0},{24,8},{1,17},{9,25},{17,1},{25,9},{2,18},{10... | collective-permute-start | bytes 1179656 | tf_op jit(solution)/shard_map/ppermute | solution.py:51
  264.3 25.5 %collective-permute-start.22 = (bf16[256,768]{1,0:T(8,128)(2,1)}, bf16[256,768]{1,0:T(8,128)(2,1)S(1)}, u32[]{:S(2)}, u32[]{:S(2)}) collective-permute-start(bf16[256,768]{1,0:T(8,128)(2,1)} %get-tuple-element.202), channel_id=1, source_target_pairs={{0,24},{8,0},{16,8},{24,16},{1,25},{9,1},{17,9},{25,17},{2,26},{10... | collective-permute-start | bytes 1179656 | tf_op jit(solution)/shard_map/ppermute | solution.py:51
  317.1 16.5 %collective-permute-start.27 = (bf16[256,768]{1,0:T(8,128)(2,1)S(1)}, bf16[256,768]{1,0:T(8,128)(2,1)S(1)}, u32[]{:S(2)}, u32[]{:S(2)}) collective-permute-start(bf16[256,768]{1,0:T(8,128)(2,1)S(1)} %copy-done.39), channel_id=1, source_target_pairs={{0,24},{8,0},{16,8},{24,16},{1,25},{9,1},{17,9},{25,17},{2,26},{10... | collective-permute-start | bytes 1179656 | tf_op jit(solution)/shard_map/ppermute | solution.py:44
  317.2 33.4 %collective-permute-start.28 = (bf16[256,768]{1,0:T(8,128)(2,1)S(1)}, bf16[256,768]{1,0:T(8,128)(2,1)S(1)}, u32[]{:S(2)}, u32[]{:S(2)}) collective-permute-start(bf16[256,768]{1,0:T(8,128)(2,1)S(1)} %copy-done.39), channel_id=1, source_target_pairs={{0,16},{8,24},{16,0},{24,8},{1,17},{9,25},{17,1},{25,9},{2,18},{10... | collective-permute-start | bytes 1179656 | tf_op jit(solution)/shard_map/ppermute | solution.py:44
  317.3 33.4 %collective-permute-start.29 = (bf16[256,768]{1,0:T(8,128)(2,1)S(1)}, bf16[256,768]{1,0:T(8,128)(2,1)S(1)}, u32[]{:S(2)}, u32[]{:S(2)}) collective-permute-start(bf16[256,768]{1,0:T(8,128)(2,1)S(1)} %copy-done.39), channel_id=1, source_target_pairs={{0,8},{8,16},{16,24},{24,0},{1,9},{9,17},{17,25},{25,1},{2,10},{10... | collective-permute-start | bytes 1179656 | tf_op jit(solution)/shard_map/ppermute | solution.py:44
  319.2 101.8 %reduce-scatter.8.cloned.1.call-start = ((), (), s32[]{:S(2)}) async-start(), calls=%async_computation.5 | async-start | bytes 1966080 | tf_op jit(solution)/shard_map/reduce_scatter | solution.py:1137
  332.1 31.7 %collective-permute-start.26 = (bf16[4,1,256,384]{3,2,0,1:T(8,128)(2,1)}, bf16[4,1,256,384]{3,2,0,1:T(8,128)(2,1)S(1)}, u32[]{:S(2)}, u32[]{:S(2)}) collective-permute-start(bf16[4,1,256,384]{3,2,0,1:T(8,128)(2,1)} %bitcast.339), channel_id=1, source_target_pairs={{1,0},{3,2},{5,4},{7,6},{9,8},{11,10},{13,12},{15,14},{17,16},{19,... | collective-permute-start | bytes 2359304 | tf_op jit(solution)/shard_map/ppermute | solution.py:1079
  389.1 18.1 %collective-permute-start.36 = (bf16[2,128,768]{2,1,0:T(8,128)(2,1)S(1)}, bf16[2,128,768]{2,1,0:T(8,128)(2,1)S(1)}, u32[]{:S(2)}, u32[]{:S(2)}) collective-permute-start(bf16[2,128,768]{2,1,0:T(8,128)(2,1)S(1)} %fusion), channel_id=1, source_target_pairs={{0,1},{1,0},{2,3},{3,2},{4,5},{5,4},{6,7},{7,6},{8,9},{9,8},{10,11... | collective-permute-start | bytes 1179656 | tf_op jit(solution)/shard_map/ppermute | solution.py:70
  389.1 17.8 %collective-permute-start.38 = (bf16[2,96,768]{2,1,0:T(8,128)(2,1)S(1)}, bf16[2,96,768]{2,1,0:T(8,128)(2,1)S(1)}, u32[]{:S(2)}, u32[]{:S(2)}) collective-permute-start(bf16[2,96,768]{2,1,0:T(8,128)(2,1)S(1)} %fusion.2), channel_id=1, source_target_pairs={{0,1},{1,0},{2,3},{3,2},{4,5},{5,4},{6,7},{7,6},{8,9},{9,8},{10,11... | collective-permute-start | bytes 884744 | tf_op jit(solution)/shard_map/ppermute | solution.py:70
  391.2 15.9 %collective-permute-start.39 = (bf16[2,104,768]{2,1,0:T(8,128)(2,1)S(1)}, bf16[2,104,768]{2,1,0:T(8,128)(2,1)S(1)}, u32[]{:S(2)}, u32[]{:S(2)}) collective-permute-start(bf16[2,104,768]{2,1,0:T(8,128)(2,1)S(1)} %fusion.1), channel_id=1, source_target_pairs={{0,4},{2,6},{4,0},{6,2},{1,5},{3,7},{5,1},{7,3},{8,12},{10,14},{12... | collective-permute-start | bytes 958472 | tf_op jit(solution)/shard_map/ppermute | solution.py:70
  (76 other events, 523.8 us)
Sparse Core Ops, SparseCore 0:
  12.3 37.0 all-gather.8
  55.7 29.4 all-gather.12
  87.6 35.7 all-gather.10
  149.6 52.6 all-gather.14
  236.6 51.2 reduce-scatter.3
  319.4 43.5 reduce-scatter.5
  382.0 33.7 reduce-scatter.7
